TPU v7x, 32 devices: a whole 2x2x4 slice. The times are simulated.
32 devices in a mesh: expert: 16 (over z, y, core), hidden: 2 (over x).
Axes of the slice: x: 2, y: 2, z: 4, core: 2. Of those that a mesh axis runs over, the one named last changes fastest.
Arguments:
- tokens: bfloat16 [2048, 4096], P('expert'), may hold values from -6 to 6
- enc_weight: bfloat16 [4096, 1024], P('expert', 'hidden'), may hold values from -0.09375 to 0.09375
- routes: int32 [2048, 8], P('expert'), may hold values from 0 to 15, all different within a row; in each aligned block of 128 rows (0 to 127, 128 to 255, ...) at most 128 rows name the same one
- gates: float32 [2048, 8], P('expert'), may hold values from 0.1 to 1
- gate_weight: bfloat16 [16, 1024, 1536], P('expert', None, 'hidden'), may hold values from -0.1875 to 0.1875
- up_weight: bfloat16 [16, 1024, 1536], P('expert', None, 'hidden'), may hold values from -0.1875 to 0.1875
- down_weight: bfloat16 [16, 1536, 1024], P('expert', None, 'hidden'), may hold values from -0.15625 to 0.15625
- dec_weight: bfloat16 [1024, 4096], P('expert', 'hidden'), may hold values from -0.1875 to 0.1875
Outputs:
- mixed: bfloat16 [2048, 4096], P('expert', 'hidden')
Inputs may be any that keep to these rules, and one draw needn't show every extreme that they name: `routes`: each row names 8 different experts; within one group of 128 consecutive tokens no expert is named more than 128 times.
All inputs are finite; a program needn't handle non-finite values.
Results may differ from a plain program's by a relative error of at most 0.0076.
Values may be sent and summed in bfloat16 or wider, within the bound.
A program may use at most 64 MiB of HBM per device.

v0:
```python
import jax
import jax.numpy as jnp
from jax import lax
from jax.experimental import pallas as pl
from jax.experimental.pallas import tpu as pltpu
from jax.sharding import PartitionSpec as P


def exchange_slots(tokens, enc_weight, routes, gates, gate_weight, up_weight, down_weight, dec_weight):
    groups = lax.axis_size("expert")
    token_count, choice_count = routes.shape
    capacity = min(token_count, 2 * token_count * choice_count // groups)
    columns = tokens
    latent = jnp.dot(
        columns,
        lax.all_gather(enc_weight, "expert", axis=0, tiled=True),
        preferred_element_type=jnp.float32,
    ).astype(jnp.bfloat16)
    payload = lax.all_gather(latent, "hidden", axis=1, tiled=True)
    chosen = routes.reshape(-1)
    onehot = (chosen[:, None] == jnp.arange(groups, dtype=jnp.int32)[None, :]).astype(jnp.int32)
    position = jnp.sum((jnp.cumsum(onehot, axis=0) - onehot) * onehot, axis=1)
    target = chosen * capacity + position
    source_row = jnp.arange(token_count * choice_count, dtype=jnp.int32) // choice_count
    payload_width = payload.shape[1]
    outgoing = (
        jnp.zeros((groups * capacity, payload_width), jnp.bfloat16)
        .at[target]
        .set(payload[source_row])
    )
    outgoing = outgoing.reshape(groups, capacity, payload_width)
    gate_matrix = gate_weight[0]
    up_matrix = up_weight[0]
    down_matrix = down_weight[0]
    arrived = lax.all_to_all(outgoing, "expert", split_axis=0, concat_axis=0, tiled=True)
    slot_count = arrived.shape[1]
    inputs = arrived.reshape(groups * slot_count, arrived.shape[2])
    gate_part = jnp.dot(inputs, gate_matrix, preferred_element_type=jnp.float32)
    up_part = jnp.dot(inputs, up_matrix, preferred_element_type=jnp.float32)
    activation = (jax.nn.silu(gate_part) * up_part).astype(jnp.bfloat16)
    answer = jnp.dot(
        lax.all_gather(activation, "hidden", axis=1, tiled=True),
        down_matrix,
        preferred_element_type=jnp.float32,
    ).astype(jnp.bfloat16)
    answer = answer.reshape(groups, slot_count, down_matrix.shape[1])
    returned_rows = lax.all_to_all(answer, "expert", split_axis=0, concat_axis=0, tiled=True)
    returned_rows = returned_rows.reshape(groups * capacity, returned_rows.shape[2])
    picked = returned_rows[target].astype(jnp.float32).reshape(token_count, choice_count, -1)
    combined = jnp.sum(picked * gates[:, :, None], axis=1).astype(jnp.bfloat16)
    combined_all = lax.all_gather(combined, "hidden", axis=1, tiled=True)
    columns = combined_all
    return jnp.dot(
        columns,
        lax.all_gather(dec_weight, "expert", axis=0, tiled=True),
        preferred_element_type=jnp.float32,
    ).astype(jnp.bfloat16)


CORES, LINES = 2, 2
MESH = pl.DeviceIdType.MESH


def layer_kernel(
    tokens_hbm, enc, routes, gates, gate_hbm, up_hbm, down_hbm, dec, out,
    tokens, gate, up, down, enc_all, dec_all, latents, own_pack, pack_all, shares, total, mixed, activation,
    answers, core_in, x_out, x_in, keep, y_out, y_in, z_out, z_in, combined,
    enc_recv, enc_send, lat_recv, lat_send, dec_recv, dec_send,
    pack_recv, pack_send,
    down_recv, down_send, core_recv, core_send, x_lat_recv, x_lat_send, core_lat_recv, core_lat_send, x_recv, x_send, y_recv, y_send,
    z_recv, z_send, last_recv, last_send, local_sem,
):
    groups = lax.axis_size("expert")
    depth = groups // (CORES * LINES)
    e = lax.axis_index("expert")
    h = lax.axis_index("hidden")
    c, y, z = e % CORES, (e // CORES) % LINES, e // (CORES * LINES)

    def at(zz, yy, cc):
        return (zz * LINES + yy) * CORES + cc

    orders = []
    for zz in range(depth):
        others = [o for o in range(depth) if o != zz]
        orders.append([zz] + sorted(others, key=lambda o: (abs(o - zz), o)))
    nearest = []
    for s in range(depth):
        pick = jnp.int32(orders[0][s])
        for zz in range(1, depth):
            pick = jnp.where(z == zz, orders[zz][s], pick)
        nearest.append(pick)

    def behind(s):
        return nearest[s]

    rows = tokens.shape[0]
    half = latents.shape[2]
    enc_rows = tokens.shape[1] // groups
    band = LINES * CORES * rows
    y_peer = (at(z, 1 - y, c), h)
    core_peer = (at(z, y, 1 - c), h)
    x_peer = (e, 1 - h)
    z_peers = [(at((z + s) % depth, y, c), h) for s in range(1, depth)]
    above = (at(jnp.minimum(z + 1, depth - 1), y, c), h)
    below = (at(jnp.maximum(z - 1, 0), y, c), h)
    has_above, has_below = z < depth - 1, z > 0

    waiting = []

    def send(src, dst, ssem, rsem, peer, when=None):
        copy = pltpu.make_async_remote_copy(
            src_ref=src, dst_ref=dst, send_sem=ssem, recv_sem=rsem,
            device_id=peer, device_id_type=MESH,
        )
        if when is None:
            copy.start()
        else:
            pl.when(when)(copy.start)
        waiting.append((copy, when))

    def arrive(dst, rsem):
        pltpu.make_async_copy(dst, dst, rsem).wait()

    barrier = pltpu.get_barrier_semaphore()
    peers = z_peers + [y_peer, core_peer, x_peer]
    for peer in peers:
        pl.semaphore_signal(barrier, inc=1, device_id=peer, device_id_type=MESH)
    pl.semaphore_wait(barrier, len(peers))

    class Gather:
        def __init__(self, own, block, rsem, ssem):
            self.own, self.block, self.rsem, self.ssem = own, block, rsem, ssem

        def forward(self, o, peer, slot, own=False, when=None):
            src = self.own if own else self.block(o)
            send(src, self.block(o), self.ssem.at[slot], self.rsem.at[o], peer, when)

        def wait(self, o):
            arrive(self.block(o), self.rsem.at[o])

        def start_z(self):
            self.forward(e, above, 0, True, has_above)
            self.forward(e, below, 1, True, has_below)

        def start_y(self):
            self.forward(e, y_peer, depth + 1, True)
            self.forward(e, core_peer, 2 * depth + 1, True)

        def from_z(self, s):
            zz = nearest[s]
            o = at(zz, y, c)
            self.wait(o)
            self.forward(o, above, s + 1, False, jnp.logical_and(zz < z, has_above))
            self.forward(o, below, s + 1, False, jnp.logical_and(zz > z, has_below))
            self.forward(o, y_peer, depth + 1 + s)
            self.forward(o, core_peer, 2 * depth + 1 + s)
            return o

        def from_y(self, s):
            o = at(nearest[s], 1 - y, c)
            self.wait(o)
            self.forward(o, core_peer, 3 * depth + 1 + s)
            return o

        def from_core(self, s, yy):
            o = at(nearest[s], yy, 1 - c)
            self.wait(o)
            return o

    def lat_block(o):
        return latents.at[h, pl.ds(pl.multiple_of(o * rows, rows), rows)]

    class LatentGather(Gather):
        def start_y(self):
            Gather.start_y(self)
            send(lat(h, e), lat(h, e), x_lat_send.at[0], x_lat_recv.at[e], x_peer)

        def from_z(self, s):
            o = Gather.from_z(self, s)
            send(lat(h, o), lat(h, o), x_lat_send.at[s], x_lat_recv.at[o], x_peer)

        def from_y(self, s):
            o = Gather.from_y(self, s)
            send(lat(h, o), lat(h, o), x_lat_send.at[depth + s], x_lat_recv.at[o], x_peer)

    enc_gather = Gather(enc, lambda o: enc_all.at[o], enc_recv, enc_send)
    dec_gather = Gather(dec, lambda o: dec_all.at[o], dec_recv, dec_send)
    pack_gather = Gather(own_pack, lambda o: pack_all.at[o], pack_recv, pack_send)
    enc_gather.start_z()
    enc_gather.start_y()

    local = [
        pltpu.make_async_copy(tokens_hbm, tokens, local_sem.at[0]),
        pltpu.make_async_copy(gate_hbm.at[0], gate, local_sem.at[1]),
        pltpu.make_async_copy(up_hbm.at[0], up, local_sem.at[2]),
    ]
    for copy in local:
        copy.start()
    part = down.shape[1]
    own_down = pltpu.make_async_copy(
        down_hbm.at[0, pl.ds(pl.multiple_of(h * part, part), part)], down.at[h], local_sem.at[3]
    )
    own_down.start()
    send(
        down_hbm.at[0, pl.ds(pl.multiple_of((1 - h) * part, part), part)],
        down.at[h], down_send.at[0], down_recv.at[0], x_peer,
    )

    local[0].wait()

    def enc_dot(o, block):
        columns = pl.ds(pl.multiple_of(o * enc_rows, enc_rows), enc_rows)
        return jnp.dot(tokens[:, columns], block, preferred_element_type=jnp.float32)

    lane = lax.broadcasted_iota(jnp.int32, (rows, 128), 1)
    weight = jnp.zeros((rows, 128), jnp.float32)
    for k in range(routes.shape[1]):
        weight += jnp.where(routes[:, k : k + 1] == lane % groups, gates[:, k : k + 1], 0.0)
    first = weight.astype(jnp.bfloat16).astype(jnp.float32)
    second = (weight - first).astype(jnp.bfloat16).astype(jnp.float32)
    piece = jnp.where(lane < groups, first, jnp.where(lane < 2 * groups, second, weight - first - second))
    own_pack[...] = piece.astype(jnp.bfloat16)

    def take_shares(o, block):
        mine = jnp.logical_and(lane % groups == e, lane < 3 * groups)
        summed = jnp.sum(jnp.where(mine, block.astype(jnp.float32), 0.0), axis=1, keepdims=True)
        start = pl.multiple_of(o * rows, rows)
        shares[pl.ds(start, rows), :] = jnp.broadcast_to(summed, (rows, 128))

    total[...] = enc_dot(e, enc[...])
    take_shares(e, own_pack[...])

    def landed(o):
        total[...] += enc_dot(o, enc_all[o])

    for s in range(1, depth + 1):
        if s < depth:
            o = enc_gather.from_z(s)
            if s == depth - 1:
                dec_gather.start_z()
            landed(o)
        landed(enc_gather.from_y(s - 1))
        landed(enc_gather.from_core(s - 1, y))
        if s >= 2:
            landed(enc_gather.from_core(s - 2, 1 - y))
    landed(enc_gather.from_core(depth - 1, 1 - y))

    def lat(hh, o):
        return latents.at[hh, pl.ds(pl.multiple_of(o * rows, rows), rows)]

    lat_gather = LatentGather(lat_block(e), lat_block, lat_recv, lat_send)
    latents[h, pl.ds(pl.multiple_of(e * rows, rows), rows), :] = total[...].astype(jnp.bfloat16)
    lat_gather.start_z()
    lat_gather.start_y()
    pack_gather.start_z()
    pack_gather.start_y()

    def lat_x(s):
        for k, yy in enumerate((y, 1 - y)):
            o = at(nearest[s], yy, c)
            arrive(lat(1 - h, o), x_lat_recv.at[o])
            send(lat(1 - h, o), lat(1 - h, o), core_lat_send.at[k * depth + s], core_lat_recv.at[o], core_peer)

    def lat_core(s):
        for yy in (y, 1 - y):
            o = lat_gather.from_core(s, yy)
            arrive(lat(1 - h, o), core_lat_recv.at[o])
            pack_gather.from_core(s, yy)
            take_shares(o, pack_all[o])

    tile = 256

    def gate_up(s, slot):
        start = pl.multiple_of(behind(s) * band, band)

        @pl.loop(0, gate.shape[1] // tile)
        def _(n):
            columns = pl.ds(pl.multiple_of(n * tile, tile), tile)
            low, high = latents[0, pl.ds(start, band), :], latents[1, pl.ds(start, band), :]
            g = jnp.dot(low, gate[:half, columns], preferred_element_type=jnp.float32)
            g += jnp.dot(high, gate[half:, columns], preferred_element_type=jnp.float32)
            u = jnp.dot(low, up[:half, columns], preferred_element_type=jnp.float32)
            u += jnp.dot(high, up[half:, columns], preferred_element_type=jnp.float32)
            activation[slot, :, columns] = (g / (1.0 + jnp.exp(-g)) * u).astype(jnp.bfloat16)

    def down_rows(s, slot, cc):
        blocks = [yy * CORES + cc for yy in range(LINES)]
        for hh in range(2):
            @pl.loop(0, half // tile)
            def _(n):
                columns = pl.ds(pl.multiple_of(n * tile, tile), tile)
                picked = [activation[slot, pl.ds(pl.multiple_of(b * rows, rows), rows), :] for b in blocks]
                a = jnp.dot(
                    jnp.concatenate(picked, axis=0), down[hh, :, columns],
                    preferred_element_type=jnp.float32,
                )
                for k, b in enumerate(blocks):
                    start = pl.multiple_of(behind(s) * band + b * rows, rows)
                    share = shares[pl.ds(start, rows), 0:1]
                    answers[s, b, hh, :, columns] = (a[k * rows : (k + 1) * rows] * share).astype(jnp.bfloat16)

    def answer_rows(s, slot):
        down_rows(s, slot, 1 - c)
        for yy in range(LINES):
            send(
                answers.at[s, yy * CORES + 1 - c], core_in.at[s, yy],
                core_send.at[s, yy], core_recv.at[s, yy], core_peer,
            )
        down_rows(s, slot, c)

    def sum_cores(s):
        for yy in range(LINES):
            arrive(core_in.at[s, yy], core_recv.at[s, yy])
        for yy in (1 - y, y):
            mine = yy * CORES + c
            other = answers[s, mine, 1 - h].astype(jnp.float32)
            x_out[s, yy] = (other + core_in[s, yy, 1 - h].astype(jnp.float32)).astype(jnp.bfloat16)
            send(x_out.at[s, yy], x_in.at[s, yy], x_send.at[s, yy], x_recv.at[s, yy], x_peer)
        for yy in range(LINES):
            mine = yy * CORES + c
            keep[s, yy] = answers[s, mine, h].astype(jnp.float32) + core_in[s, yy, h].astype(jnp.float32)

    def sum_x(s):
        arrive(x_in.at[s, 1 - y], x_recv.at[s, 1 - y])
        y_out[s] = (keep[s, 1 - y] + x_in[s, 1 - y].astype(jnp.float32)).astype(jnp.bfloat16)
        send(y_out.at[s], y_in.at[s], y_send.at[s], y_recv.at[s], y_peer)
        arrive(x_in.at[s, y], x_recv.at[s, y])
        keep[s, y] = keep[s, y] + x_in[s, y].astype(jnp.float32)

    def sum_y(s):
        arrive(y_in.at[s], y_recv.at[s])
        total = keep[s, y] + y_in[s].astype(jnp.float32)
        if s == 0:
            keep[s, y] = total
        else:
            z_out[s] = total.astype(jnp.bfloat16)
            peer = (at(behind(s), y, c), h)
            send(z_out.at[s], z_in.at[z], z_send.at[s], z_recv.at[z], peer)

    def pack_z(s):
        take_shares(pack_gather.from_z(s), pack_all[at(nearest[s], y, c)])

    def pack_y(s):
        take_shares(pack_gather.from_y(s), pack_all[at(nearest[s], 1 - y, c)])

    for s in range(1, depth + 1):
        if s < depth:
            lat_gather.from_z(s)
        lat_gather.from_y(s - 1)
        if s < depth:
            pack_z(s)
        pack_y(s - 1)
    dec_gather.start_y()
    local[1].wait()
    local[2].wait()
    own_down.wait()
    arrive(down.at[1 - h], down_recv.at[0])
    last = depth - 1
    dec_gather.from_z(1)
    lat_x(0)
    lat_core(0)
    gate_up(0, 0)
    lat_x(1)
    lat_core(1)
    for s in range(1, depth):
        gate_up(s, 1)
        if s < last:
            lat_x(s + 1)
        answer_rows(s, 1)
        sum_cores(s)
        if s < last:
            lat_core(s + 1)
        if s >= 2:
            sum_x(s - 1)
        if s >= 3:
            sum_y(s - 2)
        if s < last:
            dec_gather.from_z(s + 1)
    answer_rows(0, 0)
    sum_cores(0)
    if last >= 2:
        sum_y(last - 1)
    sum_x(last)
    for s in range(depth):
        dec_gather.from_y(s)
    sum_y(last)
    sum_x(0)
    final = jnp.zeros((rows, half), jnp.float32)
    for s in range(1, depth):
        arrive(z_in.at[nearest[s]], z_recv.at[nearest[s]])
        final += z_in[nearest[s]].astype(jnp.float32)
    total[...] = final
    for s in range(depth):
        for yy in (y, 1 - y):
            dec_gather.from_core(s, yy)
    dec_all[e] = dec[...]
    sum_y(0)
    combined[h] = (total[...] + keep[0, y]).astype(jnp.bfloat16)
    send(combined.at[h], combined.at[h], last_send.at[0], last_recv.at[0], x_peer)

    per = groups // 2

    def product(hh, columns):
        part = dec_all[pl.ds(pl.multiple_of(hh * per, per), per), :, columns].reshape(half, tile)
        return jnp.dot(combined[hh], part, preferred_element_type=jnp.float32)

    @pl.loop(0, out.shape[1] // tile)
    def _(n):
        columns = pl.ds(pl.multiple_of(n * tile, tile), tile)
        mixed[:, columns] = product(h, columns)

    arrive(combined.at[1 - h], last_recv.at[0])

    @pl.loop(0, out.shape[1] // tile)
    def _(n):
        columns = pl.ds(pl.multiple_of(n * tile, tile), tile)
        out[:, columns] = (mixed[:, columns] + product(1 - h, columns)).astype(jnp.bfloat16)

    for copy, when in waiting:
        if when is None:
            copy.wait_send()
        else:
            pl.when(when)(copy.wait_send)


def whole_layer(tokens, enc_weight, routes, gates, gate_weight, up_weight, down_weight, dec_weight):
    groups = lax.axis_size("expert")
    depth = groups // (CORES * LINES)
    rows, width = tokens.shape
    half = enc_weight.shape[1]
    hidden = gate_weight.shape[2]
    bf, f32 = jnp.bfloat16, jnp.float32
    band = LINES * CORES
    anywhere = pl.BlockSpec(memory_space=pl.ANY)
    vmem = pl.BlockSpec(memory_space=pltpu.VMEM)
    dma = pltpu.SemaphoreType.DMA
    scratch = [
        pltpu.VMEM((rows, width), bf),
        pltpu.VMEM(gate_weight.shape[1:], bf),
        pltpu.VMEM(up_weight.shape[1:], bf),
        pltpu.VMEM((2, hidden, half), bf),
        pltpu.VMEM((groups, *enc_weight.shape), bf),
        pltpu.VMEM((groups, *dec_weight.shape), bf),
        pltpu.VMEM((2, groups * rows, half), bf),
        pltpu.VMEM((rows, 128), bf),
        pltpu.VMEM((groups, rows, 128), bf),
        pltpu.VMEM((groups * rows, 128), f32),
        pltpu.VMEM((rows, half), f32),
        pltpu.VMEM((rows, dec_weight.shape[1]), f32),
        pltpu.VMEM((2, band * rows, hidden), bf),
        pltpu.VMEM((depth, band, 2, rows, half), bf),
        pltpu.VMEM((depth, LINES, 2, rows, half), bf),
        pltpu.VMEM((depth, LINES, rows, half), bf),
        pltpu.VMEM((depth, LINES, rows, half), bf),
        pltpu.VMEM((depth, LINES, rows, half), f32),
        pltpu.VMEM((depth, rows, half), bf),
        pltpu.VMEM((depth, rows, half), bf),
        pltpu.VMEM((depth, rows, half), bf),
        pltpu.VMEM((depth, rows, half), bf),
        pltpu.VMEM((2, rows, half), bf),
        *[dma((groups,)), dma((4 * depth + 1,))] * 4,
        dma((1,)), dma((1,)),
        dma((depth, LINES)), dma((depth, LINES)),
        dma((groups,)), dma((2 * depth,)), dma((groups,)), dma((2 * depth,)),
        dma((depth, LINES)), dma((depth, LINES)), dma((depth,)), dma((depth,)), dma((depth,)), dma((depth,)),
        dma((1,)), dma((1,)), dma((4,)),
    ]
    return pl.pallas_call(
        layer_kernel,
        out_shape=jax.ShapeDtypeStruct((rows, dec_weight.shape[1]), bf),
        in_specs=[anywhere, vmem, vmem, vmem, anywhere, anywhere, anywhere, vmem],
        out_specs=vmem,
        scratch_shapes=scratch,
        compiler_params=pltpu.CompilerParams(
            collective_id=0, has_side_effects=True, vmem_limit_bytes=60 * 1024 * 1024
        ),
    )(tokens, enc_weight, routes, gates, gate_weight, up_weight, down_weight, dec_weight)


def on_device(tokens, enc_weight, routes, *rest):
    token_count, choice_count = routes.shape
    plan = whole_layer if 2 * choice_count >= lax.axis_size("expert") else exchange_slots
    return plan(tokens, enc_weight, routes, *rest)


def solution(mesh):
    in_specs = (
        P("expert", None),
        P("expert", "hidden"),
        P("expert", None),
        P("expert", None),
        P("expert", None, "hidden"),
        P("expert", None, "hidden"),
        P("expert", None, "hidden"),
        P("expert", "hidden"),
    )
    out_specs = P("expert", "hidden")
    return jax.shard_map(
        on_device, mesh=mesh, in_specs=in_specs, out_specs=out_specs, check_vma=False
    )
```

profile of v0, /device:TPU:0, one launch (start us, length us, event | category | flops | bytes accessed | tf_op | source)
XLA Modules:
  0.0 112.7 jit_solution(8674855723731702664)
XLA Ops:
  0.0 1.4 %copy.9.routes = s32[128,8]{1,0:T(8,128)} copy(s32[128,8]{0,1:T(8,128)} %param.10) | data formatting | bytes 8192 | tf_op args[2]
  1.4 1.4 %copy.10.gates = f32[128,8]{1,0:T(8,128)} copy(f32[128,8]{0,1:T(8,128)} %param.11) | data formatting | bytes 8192 | tf_op args[3]
  2.8 108.0 %shard_map.82 = bf16[128,2048]{1,0:T(8,128)(2,1)} custom-call(bf16[128,4096]{1,0:T(8,128)(2,1)} %tokens_hbm.1, bf16[256,512]{1,0:T(8,128)(2,1)} %enc.1, s32[128,8]{1,0:T(8,128)} %copy.9.routes, f32[128,8]{1,0:T(8,128)} %copy.10.gates, bf16[1,1024,768]{2,1,0:T(8,128)(2,1)} %gate_hbm.1, bf16[1,1024,768]{2,1,0:T(8,128)(2,1)} %up_hbm.1, ...), custom_call_target="tpu_custom_call" | custom-call | tf_op jit(solution)/shard_map/pallas_call | solution.py:468
  110.9 1.9 %copy.12 = bf16[128,2048]{1,0:T(8,128)(2,1)} copy(bf16[128,2048]{1,0:T(8,128)(2,1)} %shard_map.82) | data formatting | bytes 1048576
where the time goes:
time: 113 us
  Pallas kernels  108 us (96%)
  local copies, waits for them, and re-layouts  4.7 us (4%)
    pallas_call x1, Pallas kernels, whole_layer(): pl.pallas_call(layer_kernel, out_shape=jax.ShapeDtypeStruct((rows, dec_we...  108 us
    unnamed x3, local copies, waits for them, and re-layouts  4.7 us

commit v1 on v0

v1 whole, which is shorter than its diff:
```python
import jax
import jax.numpy as jnp
from jax import lax
from jax.experimental import pallas as pl
from jax.experimental.pallas import tpu as pltpu
from jax.sharding import PartitionSpec as P


def exchange_slots(tokens, enc_weight, routes, gates, gate_weight, up_weight, down_weight, dec_weight):
    groups = lax.axis_size("expert")
    token_count, choice_count = routes.shape
    capacity = min(token_count, 2 * token_count * choice_count // groups)
    columns = tokens
    latent = jnp.dot(
        columns,
        lax.all_gather(enc_weight, "expert", axis=0, tiled=True),
        preferred_element_type=jnp.float32,
    ).astype(jnp.bfloat16)
    payload = lax.all_gather(latent, "hidden", axis=1, tiled=True)
    chosen = routes.reshape(-1)
    onehot = (chosen[:, None] == jnp.arange(groups, dtype=jnp.int32)[None, :]).astype(jnp.int32)
    position = jnp.sum((jnp.cumsum(onehot, axis=0) - onehot) * onehot, axis=1)
    target = chosen * capacity + position
    source_row = jnp.arange(token_count * choice_count, dtype=jnp.int32) // choice_count
    payload_width = payload.shape[1]
    outgoing = (
        jnp.zeros((groups * capacity, payload_width), jnp.bfloat16)
        .at[target]
        .set(payload[source_row])
    )
    outgoing = outgoing.reshape(groups, capacity, payload_width)
    gate_matrix = gate_weight[0]
    up_matrix = up_weight[0]
    down_matrix = down_weight[0]
    arrived = lax.all_to_all(outgoing, "expert", split_axis=0, concat_axis=0, tiled=True)
    slot_count = arrived.shape[1]
    inputs = arrived.reshape(groups * slot_count, arrived.shape[2])
    gate_part = jnp.dot(inputs, gate_matrix, preferred_element_type=jnp.float32)
    up_part = jnp.dot(inputs, up_matrix, preferred_element_type=jnp.float32)
    activation = (jax.nn.silu(gate_part) * up_part).astype(jnp.bfloat16)
    answer = jnp.dot(
        lax.all_gather(activation, "hidden", axis=1, tiled=True),
        down_matrix,
        preferred_element_type=jnp.float32,
    ).astype(jnp.bfloat16)
    answer = answer.reshape(groups, slot_count, down_matrix.shape[1])
    returned_rows = lax.all_to_all(answer, "expert", split_axis=0, concat_axis=0, tiled=True)
    returned_rows = returned_rows.reshape(groups * capacity, returned_rows.shape[2])
    picked = returned_rows[target].astype(jnp.float32).reshape(token_count, choice_count, -1)
    combined = jnp.sum(picked * gates[:, :, None], axis=1).astype(jnp.bfloat16)
    combined_all = lax.all_gather(combined, "hidden", axis=1, tiled=True)
    columns = combined_all
    return jnp.dot(
        columns,
        lax.all_gather(dec_weight, "expert", axis=0, tiled=True),
        preferred_element_type=jnp.float32,
    ).astype(jnp.bfloat16)


CORES, LINES = 2, 2
MESH = pl.DeviceIdType.MESH


CHUNKS, PIECES = 2, 4
LATENT_FIRST = ((1, 0), (1, 0), (1, 0), (1, 0))
ANSWER_FIRST = ((0, 0), (0, 0), (0, 0), (0, 0))


def layer_kernel(
    tokens_hbm, enc_hbm, routes, gates, gate_hbm, up_hbm, down_hbm, dec_hbm, out,
    tok, gate, up, down, enc_all, dec_all, latents, table, shares_in, shares, acc, part_out, part_in, activation,
    answers, core_in, one_out, one_in, two_out, two_in, keep, z_out, z_in, combined, mixed, result,
    ssem, rsem, enc_z, lat_z, share_sem, dec_sem, z_sem, local_sem,
):
    groups = lax.axis_size("expert")
    depth = groups // (CORES * LINES)
    e = lax.axis_index("expert")
    h = lax.axis_index("hidden")
    c, y, z = e % CORES, (e // CORES) % LINES, e // (CORES * LINES)

    def at(zz, yy, cc):
        return (zz * LINES + yy) * CORES + cc

    orders = []
    for zz in range(depth):
        others = [o for o in range(depth) if o != zz]
        middle = (depth - 1) / 2
        orders.append([zz] + sorted(others, key=lambda o: (abs(o - zz), abs(o - middle))))
    nearest = []
    for s in range(depth):
        pick = jnp.int32(orders[0][s])
        for zz in range(1, depth):
            pick = jnp.where(z == zz, orders[zz][s], pick)
        nearest.append(pick)

    rows = tok.shape[1] // 2
    wide = tok.shape[2]
    chunk = latents.shape[3]
    half = chunk * CHUNKS
    band = LINES * CORES * rows
    last = depth - 1
    y_peer = (at(z, 1 - y, c), h)
    core_peer = (at(z, y, 1 - c), h)
    x_peer = (e, 1 - h)

    def route(pair, cc):
        along_y = jnp.where(cc == 0, pair[0], pair[1]) == 1
        first = (jnp.where(along_y, at(z, 1 - y, c), e), jnp.where(along_y, h, 1 - h))
        second = (jnp.where(along_y, e, at(z, 1 - y, c)), jnp.where(along_y, 1 - h, h))
        f = (jnp.where(along_y, 1 - y, y), jnp.where(along_y, h, 1 - h))
        g = (jnp.where(along_y, y, 1 - y), jnp.where(along_y, 1 - h, h))
        return first, second, f, g

    waiting, slots, local = [], {}, []

    def slot(*key):
        return rsem.at[slots.setdefault(key, len(slots))]

    def send(src, dst, sem, peer, when=None):
        copy = pltpu.make_async_remote_copy(
            src_ref=src, dst_ref=dst, send_sem=ssem.at[len(waiting)], recv_sem=sem,
            device_id=peer, device_id_type=MESH,
        )
        if when is None:
            copy.start()
        else:
            pl.when(when)(copy.start)
        waiting.append((copy, when))

    def along(zz):
        return (at(jnp.clip(zz, 0, depth - 1), y, c), h)

    ending = jnp.logical_or(z == 0, z == depth - 1)

    def spread(block, sem, far=(1, 2), when=True):
        for d in far:
            send(block, block, sem, along(z + d), jnp.logical_and(when, z + d < depth))
            send(block, block, sem, along(z - d), jnp.logical_and(when, z - d >= 0))

    def hand_on(block, sem, zz):
        send(block, block, sem, along(z + 1), jnp.logical_and(z - zz == 2, z + 1 < depth))
        send(block, block, sem, along(z - 1), jnp.logical_and(zz - z == 2, z - 1 >= 0))

    def arrive(dst, sem):
        pltpu.make_async_copy(dst, dst, sem).wait()

    def fetch(src, dst):
        copy = pltpu.make_async_copy(src, dst, local_sem.at[len(local)])
        copy.start()
        local.append(copy)
        return copy

    barrier = pltpu.get_barrier_semaphore()
    peers = [((e + d) % groups, h) for d in range(1, groups)] + [x_peer]
    for peer in peers:
        pl.semaphore_signal(barrier, inc=1, device_id=peer, device_id_type=MESH)

    def segment(zz, yy):
        return pl.ds(pl.multiple_of((zz * LINES + yy) * wide, wide), wide)

    enc_own = [
        fetch(enc_hbm.at[:, pl.ds(k * chunk, chunk)], enc_all.at[k, z, c]) for k in range(CHUNKS)
    ]
    tok_own = [fetch(tokens_hbm.at[:, segment(zz, y)], tok.at[zz, pl.ds(0, rows)]) for zz in range(depth)]
    dec_own = fetch(dec_hbm, dec_all.at[e])
    part = down.shape[1]
    gate_own = fetch(gate_hbm.at[0], gate)
    up_own = fetch(up_hbm.at[0], up)
    own_down = fetch(down_hbm.at[0, pl.ds(pl.multiple_of(h * part, part), part)], down.at[h])

    expert = lax.broadcasted_iota(jnp.int32, (groups, rows), 0)
    weight = jnp.zeros((groups, rows), jnp.float32)
    for k in range(routes.shape[0]):
        weight += jnp.where(routes[k : k + 1, :] == expert, gates[k : k + 1, :], 0.0)
    for o in range(groups):
        table[o] = jnp.broadcast_to(weight[o : o + 1, :], table.shape[1:])

    pl.semaphore_wait(barrier, len(peers))

    def enc_block(k, zz, cc):
        return enc_all.at[k, zz, cc]

    def enc_start(k):
        block = enc_block(k, z, c)
        enc_own[k].wait()
        if k == 0:
            spread(block, enc_z.at[k, z])
        else:
            spread(block, enc_z.at[k, z], (1,))
            spread(block, enc_z.at[k, z], (2,), ending)
        send(block, block, slot("enc", k, 0), core_peer)

    def enc_later(k):
        spread(enc_block(k, z, c), enc_z.at[k, z], (2,), jnp.logical_not(ending))

    def enc_from_z(k, s):
        zz = nearest[s]
        block = enc_block(k, zz, c)
        arrive(block, enc_z.at[k, zz])
        if s == last:
            hand_on(block, enc_z.at[k, zz], zz)
        send(block, block, slot("enc", k, s), core_peer)

    def tok_block(zz):
        return tok.at[zz, pl.ds(rows, rows)]

    def tok_send(s):
        zz = nearest[s]
        send(tokens_hbm.at[:, segment(zz, 1 - y)], tok_block(zz), slot("tok", s), y_peer)

    def tok_wait(s):
        arrive(tok_block(nearest[s]), slot("tok", s))

    def enc_step(k, s):
        zz = nearest[s]
        arrive(enc_block(k, zz, 1 - c), slot("enc", k, s))
        p = jnp.dot(tok[zz], enc_all[k, zz].reshape(wide, chunk), preferred_element_type=jnp.float32)
        if s == 0:
            acc[k] = p
        else:
            acc[k] = acc[k] + p

    def enc_share(k):
        part_out[k] = acc[k, rows:, :].astype(jnp.bfloat16)
        send(part_out.at[k], part_in.at[k], slot("part", k), y_peer)

    def lat_block(k, zz, yy, cc, hh):
        return latents.at[hh, k, pl.ds(pl.multiple_of(at(zz, yy, cc) * rows, rows), rows)]

    def enc_done(k):
        arrive(part_in.at[k], slot("part", k))
        own = acc[k, :rows, :] + part_in[k].astype(jnp.float32)
        latents[h, k, pl.ds(pl.multiple_of(e * rows, rows), rows), :] = own.astype(jnp.bfloat16)

    def lat_from_z(k, s):
        zz = nearest[s]
        block = lat_block(k, zz, y, c, h)
        if s == 0:
            spread(block, lat_z.at[k, zz])
        else:
            arrive(block, lat_z.at[k, zz])
            if s == last:
                hand_on(block, lat_z.at[k, zz], zz)
        first, second, _, _ = route(LATENT_FIRST[s % 4], c)
        send(block, block, slot("lat1", k, s), first)
        send(block, block, slot("lat2", k, s), second)
        send(block, block, slot("lat3", k, s, 0), core_peer)

    def lat_from_first(k, s):
        _, second, f, _ = route(LATENT_FIRST[s % 4], c)
        block = lat_block(k, nearest[s], f[0], c, f[1])
        arrive(block, slot("lat1", k, s))
        send(block, block, slot("lat4", k, s), second)
        send(block, block, slot("lat3", k, s, 1), core_peer)

    def lat_from_second(k, s):
        _, _, _, g = route(LATENT_FIRST[s % 4], c)
        block = lat_block(k, nearest[s], g[0], c, g[1])
        arrive(block, slot("lat2", k, s))
        send(block, block, slot("lat3", k, s, 2), core_peer)
        block = lat_block(k, nearest[s], 1 - y, c, 1 - h)
        arrive(block, slot("lat4", k, s))
        send(block, block, slot("lat3", k, s, 3), core_peer)

    def lat_from_core(k, s):
        _, _, f, g = route(LATENT_FIRST[s % 4], 1 - c)
        for i, (yy, hh) in enumerate(((y, h), f, g, (1 - y, 1 - h))):
            arrive(lat_block(k, nearest[s], yy, 1 - c, hh), slot("lat3", k, s, i))

    def dec_block(o):
        return dec_all.at[o]

    def dec_send(o, peer):
        send(dec_block(o), dec_block(o), dec_sem.at[o], peer)

    def dec_start_z():
        spread(dec_block(e), dec_sem.at[e])

    def dec_start_y():
        dec_own.wait()
        dec_send(e, y_peer)
        dec_send(e, core_peer)

    def dec_from_z(s):
        zz = nearest[s]
        o = at(zz, y, c)
        arrive(dec_block(o), dec_sem.at[o])
        if s == last:
            hand_on(dec_block(o), dec_sem.at[o], zz)
        dec_send(o, y_peer)
        dec_send(o, core_peer)

    def dec_from_y(s):
        o = at(nearest[s], 1 - y, c)
        arrive(dec_block(o), dec_sem.at[o])
        dec_send(o, core_peer)

    def dec_from_core(s):
        for yy in (y, 1 - y):
            o = at(nearest[s], yy, 1 - c)
            arrive(dec_block(o), dec_sem.at[o])

    piece = part // PIECES

    def down_rows(hh, i, base):
        return pl.ds(pl.multiple_of(base * part + i * piece, piece), piece)

    def down_send(i):
        send(
            down_hbm.at[0, down_rows(h, i, 1 - h)], down.at[h, pl.ds(i * piece, piece)],
            slot("down", i), x_peer,
        )

    def down_wait():
        own_down.wait()
        for i in range(PIECES):
            arrive(down.at[1 - h, pl.ds(i * piece, piece)], slot("down", i))

    def share_start():
        for d in range(1, groups):
            o = (e + d) % groups
            send(table.at[o], shares_in.at[e], share_sem.at[e], (o, h))
        shares_in[e] = table[e]

    def share_done():
        for d in range(1, groups):
            o = (e + d) % groups
            arrive(shares_in.at[o], share_sem.at[o])
        tiles = [shares_in[nearest[s] * LINES * CORES + b] for s in range(depth) for b in range(LINES * CORES)]
        shares[...] = jnp.concatenate(tiles, axis=0).T

    tile = 256

    def gate_up(s, where):
        start = pl.multiple_of(nearest[s] * band, band)

        @pl.loop(0, gate.shape[1] // tile)
        def _(n):
            columns = pl.ds(pl.multiple_of(n * tile, tile), tile)
            parts = [latents[hh, k, pl.ds(start, band), :] for hh in range(2) for k in range(CHUNKS)]
            inputs = jnp.concatenate(parts, axis=1)
            g = jnp.dot(inputs, gate[:, columns], preferred_element_type=jnp.float32)
            u = jnp.dot(inputs, up[:, columns], preferred_element_type=jnp.float32)
            activation[where, :, columns] = (g / (1.0 + jnp.exp(-g)) * u).astype(jnp.bfloat16)

    def answer_rows(s, where):
        for hh in (1 - h, h):
            @pl.loop(0, half // tile)
            def _(n):
                columns = pl.ds(pl.multiple_of(n * tile, tile), tile)
                a = jnp.dot(activation[where], down[hh, :, columns], preferred_element_type=jnp.float32)
                for b in range(LINES * CORES):
                    j = (s * LINES * CORES + b) * 8
                    share = shares[:, j : j + 1]
                    answers[s, b, hh, :, columns] = (a[b * rows : (b + 1) * rows] * share).astype(jnp.bfloat16)

            for yy in range(LINES):
                send(
                    answers.at[s, yy * CORES + 1 - c, hh], core_in.at[s, yy, hh],
                    slot("core", s, yy, 0 if hh is not h else 1), core_peer,
                )

    def both(s, yy, hh):
        return answers[s, yy * CORES + c, hh].astype(jnp.float32) + core_in[s, yy, hh].astype(jnp.float32)

    def sum_cores(s):
        first, _, f, _ = route(ANSWER_FIRST[s % 4], c)
        for i, hh in enumerate((1 - h, h)):
            for yy in range(LINES):
                arrive(core_in.at[s, yy, hh], slot("core", s, yy, i))
        for i, (yy, hh) in enumerate(((1 - y, 1 - h), f)):
            one_out[s, i] = both(s, yy, hh).astype(jnp.bfloat16)
            send(one_out.at[s, i], one_in.at[s, i], slot("one", s, i), first)

    def sum_first(s):
        _, second, _, g = route(ANSWER_FIRST[s % 4], c)
        arrive(one_in.at[s, 0], slot("one", s, 0))
        two_out[s] = (both(s, g[0], g[1]) + one_in[s, 0].astype(jnp.float32)).astype(jnp.bfloat16)
        send(two_out.at[s], two_in.at[s], slot("two", s), second)
        arrive(one_in.at[s, 1], slot("one", s, 1))
        keep[s] = both(s, y, h) + one_in[s, 1].astype(jnp.float32)

    def sum_second(s):
        arrive(two_in.at[s], slot("two", s))
        total = keep[s] + two_in[s].astype(jnp.float32)
        if s == 0:
            keep[s] = total
        else:
            z_out[s] = total.astype(jnp.bfloat16)
            peer = (at(nearest[s], y, c), h)
            send(z_out.at[s], z_in.at[z], z_sem.at[z], peer)

    enc_start(0)
    for s in range(depth):
        tok_send(s)
    for i in range(PIECES):
        down_send(i)
    share_start()
    enc_from_z(0, 1)
    enc_start(1)
    for copy in tok_own:
        copy.wait()
    enc_from_z(0, 2)
    tok_wait(0)
    enc_step(0, 0)
    tok_wait(1)
    enc_step(0, 1)
    enc_from_z(0, 3)
    enc_later(1)
    tok_wait(2)
    enc_step(0, 2)
    tok_wait(3)
    enc_step(0, 3)
    enc_share(0)
    dec_start_y()
    enc_from_z(1, 1)
    enc_step(1, 0)
    enc_from_z(1, 2)
    enc_step(1, 1)
    enc_step(1, 2)
    enc_done(0)
    lat_from_z(0, 0)
    enc_from_z(1, 3)
    enc_step(1, 3)
    enc_share(1)
    lat_from_z(0, 1)
    lat_from_first(0, 0)
    lat_from_z(0, 2)
    lat_from_first(0, 1)
    lat_from_second(0, 0)
    lat_from_z(0, 3)
    enc_done(1)
    lat_from_z(1, 0)
    lat_from_first(0, 2)
    lat_from_second(0, 1)
    lat_from_z(1, 1)
    lat_from_first(0, 3)
    lat_from_second(0, 2)
    lat_from_first(1, 0)
    lat_from_z(1, 2)
    lat_from_second(0, 3)
    lat_from_first(1, 1)
    lat_from_second(1, 0)
    share_done()
    gate_own.wait()
    up_own.wait()
    lat_from_z(1, 3)
    dec_start_z()
    lat_from_core(0, 0)
    lat_from_core(1, 0)
    gate_up(0, 0)
    lat_from_first(1, 2)
    lat_from_second(1, 1)
    lat_from_core(0, 1)
    lat_from_core(1, 1)
    gate_up(1, 1)
    lat_from_first(1, 3)
    lat_from_second(1, 2)
    down_wait()
    answer_rows(1, 1)
    lat_from_core(0, 2)
    lat_from_core(1, 2)
    sum_cores(1)
    gate_up(2, 1)
    lat_from_second(1, 3)
    dec_from_z(1)
    answer_rows(2, 1)
    lat_from_core(0, 3)
    lat_from_core(1, 3)
    sum_first(1)
    sum_cores(2)
    gate_up(3, 1)
    dec_from_z(2)
    sum_second(1)
    answer_rows(3, 1)
    sum_first(2)
    sum_cores(3)
    answer_rows(0, 0)
    dec_from_z(3)
    sum_second(2)
    sum_first(3)
    sum_cores(0)
    for s in range(depth):
        dec_from_y(s)
    sum_second(3)
    sum_first(0)
    final = jnp.zeros((rows, half), jnp.float32)
    for s in range(1, depth):
        arrive(z_in.at[nearest[s]], z_sem.at[nearest[s]])
        final += z_in[nearest[s]].astype(jnp.float32)
    keep[1] = final
    for s in range(depth):
        dec_from_core(s)
    sum_second(0)
    combined[h] = (keep[0] + keep[1]).astype(jnp.bfloat16)
    send(combined.at[h], combined.at[h], slot("last"), x_peer)

    per = groups // 2

    def product(hh, columns):
        block = dec_all[pl.ds(pl.multiple_of(hh * per, per), per), :, columns].reshape(half, tile)
        return jnp.dot(combined[hh], block, preferred_element_type=jnp.float32)

    @pl.loop(0, mixed.shape[1] // tile)
    def _(n):
        columns = pl.ds(pl.multiple_of(n * tile, tile), tile)
        mixed[:, columns] = product(h, columns)

    arrive(combined.at[1 - h], slot("last"))
    stored = []
    for i in range(2):
        width = mixed.shape[1] // 2

        @pl.loop(0, width // tile)
        def _(n):
            columns = pl.ds(pl.multiple_of(i * width + n * tile, tile), tile)
            result[:, columns] = (mixed[:, columns] + product(1 - h, columns)).astype(jnp.bfloat16)

        stored.append(fetch(result.at[:, pl.ds(i * width, width)], out.at[:, pl.ds(i * width, width)]))

    for copy, when in waiting:
        if when is None:
            copy.wait_send()
        else:
            pl.when(when)(copy.wait_send)
    for copy in stored:
        copy.wait()


def whole_layer(tokens, enc_weight, routes, gates, gate_weight, up_weight, down_weight, dec_weight):
    groups = lax.axis_size("expert")
    depth = groups // (CORES * LINES)
    rows, width = tokens.shape
    half = enc_weight.shape[1]
    hidden = gate_weight.shape[2]
    bf, f32 = jnp.bfloat16, jnp.float32
    band = LINES * CORES
    chunk = half // CHUNKS
    anywhere = pl.BlockSpec(memory_space=pl.ANY)
    vmem = pl.BlockSpec(memory_space=pltpu.VMEM)
    dma = pltpu.SemaphoreType.DMA
    scratch = [
        pltpu.VMEM((depth, 2 * rows, width // (LINES * depth)), bf),
        pltpu.VMEM(gate_weight.shape[1:], bf),
        pltpu.VMEM(up_weight.shape[1:], bf),
        pltpu.VMEM((2, hidden, half), bf),
        pltpu.VMEM((CHUNKS, depth, CORES, enc_weight.shape[0], chunk), bf),
        pltpu.VMEM((groups, *dec_weight.shape), bf),
        pltpu.VMEM((2, CHUNKS, groups * rows, chunk), bf),
        pltpu.VMEM((groups, 8, rows), f32),
        pltpu.VMEM((groups, 8, rows), f32),
        pltpu.VMEM((rows, groups * 8), f32),
        pltpu.VMEM((CHUNKS, 2 * rows, chunk), f32),
        pltpu.VMEM((CHUNKS, rows, chunk), bf),
        pltpu.VMEM((CHUNKS, rows, chunk), bf),
        pltpu.VMEM((2, band * rows, hidden), bf),
        pltpu.VMEM((depth, band, 2, rows, half), bf),
        pltpu.VMEM((depth, LINES, 2, rows, half), bf),
        pltpu.VMEM((depth, 2, rows, half), bf),
        pltpu.VMEM((depth, 2, rows, half), bf),
        pltpu.VMEM((depth, rows, half), bf),
        pltpu.VMEM((depth, rows, half), bf),
        pltpu.VMEM((depth, rows, half), f32),
        pltpu.VMEM((depth, rows, half), bf),
        pltpu.VMEM((depth, rows, half), bf),
        pltpu.VMEM((2, rows, half), bf),
        pltpu.VMEM((rows, dec_weight.shape[1]), f32),
        pltpu.VMEM((rows, dec_weight.shape[1]), bf),
        dma((256,)), dma((160,)), dma((CHUNKS, depth)), dma((CHUNKS, depth)),
        dma((groups,)), dma((groups,)), dma((depth,)), dma((16,)),
    ]
    return pl.pallas_call(
        layer_kernel,
        out_shape=jax.ShapeDtypeStruct((rows, dec_weight.shape[1]), bf),
        in_specs=[anywhere, anywhere, vmem, vmem, anywhere, anywhere, anywhere, anywhere],
        out_specs=anywhere,
        scratch_shapes=scratch,
        compiler_params=pltpu.CompilerParams(
            collective_id=0, has_side_effects=True, vmem_limit_bytes=60 * 1024 * 1024
        ),
    )(tokens, enc_weight, routes.T, gates.T, gate_weight, up_weight, down_weight, dec_weight)


def on_device(tokens, enc_weight, routes, *rest):
    token_count, choice_count = routes.shape
    plan = whole_layer if 2 * choice_count >= lax.axis_size("expert") else exchange_slots
    return plan(tokens, enc_weight, routes, *rest)


def solution(mesh):
    in_specs = (
        P("expert", None),
        P("expert", "hidden"),
        P("expert", None),
        P("expert", None),
        P("expert", None, "hidden"),
        P("expert", None, "hidden"),
        P("expert", None, "hidden"),
        P("expert", "hidden"),
    )
    out_specs = P("expert", "hidden")
    return jax.shard_map(
        on_device, mesh=mesh, in_specs=in_specs, out_specs=out_specs, check_vma=False
    )
```

time: 113 us -> 108 us (0.956)
  local copies, waits for them, and re-layouts: 4.7 us -> 1.88 us
  Pallas kernels: 108 us -> 106 us
    unnamed x3 -> x1, local copies, waits for them, and re-layouts: 4.7 us -> 1.88 us
    pallas_call x1, Pallas kernels: 108 us -> 106 us  [whole_layer(): pl.pallas_call(layer_kernel, out_shape=jax.ShapeDtypeStruct((rows, dec_we...]
where the time goes in v1:
time: 108 us
  Pallas kernels  106 us (98%)
  local copies, waits for them, and re-layouts  1.88 us (2%)
    pallas_call x1, Pallas kernels, whole_layer(): pl.pallas_call(layer_kernel, out_shape=jax.ShapeDtypeStruct((rows, dec_we...  106 us

profile of v1, /device:TPU:0, one launch (start us, length us, event | category | flops | bytes accessed | tf_op | source)
XLA Modules:
  0.0 107.6 jit_solution(441611034293850344)
XLA Ops:
  0.0 105.7 %shard_map.82 = bf16[128,2048]{1,0:T(8,128)(2,1)} custom-call(bf16[128,4096]{1,0:T(8,128)(2,1)} %tokens_hbm.1, bf16[256,512]{1,0:T(8,128)(2,1)} %enc_hbm.1, s32[8,128]{1,0:T(8,128)} %bitcast.2, f32[8,128]{1,0:T(8,128)} %bitcast.3, bf16[1,1024,768]{2,1,0:T(8,128)(2,1)} %gate_hbm.1, bf16[1,1024,768]{2,1,0:T(8,128)(2,1)} %up_hbm.1, ...), custom_call_target="tpu_custom_call" | custom-call | tf_op jit(solution)/shard_map/pallas_call | solution.py:572
  105.7 1.9 %copy.10 = bf16[128,2048]{1,0:T(8,128)(2,1)} copy(bf16[128,2048]{1,0:T(8,128)(2,1)} %shard_map.82) | data formatting | bytes 1048576

commit v2 on v1

v2 whole, which is shorter than its diff:
```python
import jax
import jax.numpy as jnp
from jax import lax
from jax.experimental import pallas as pl
from jax.experimental.pallas import tpu as pltpu
from jax.sharding import PartitionSpec as P


def exchange_slots(tokens, enc_weight, routes, gates, gate_weight, up_weight, down_weight, dec_weight):
    groups = lax.axis_size("expert")
    token_count, choice_count = routes.shape
    capacity = min(token_count, 2 * token_count * choice_count // groups)
    columns = tokens
    latent = jnp.dot(
        columns,
        lax.all_gather(enc_weight, "expert", axis=0, tiled=True),
        preferred_element_type=jnp.float32,
    ).astype(jnp.bfloat16)
    payload = lax.all_gather(latent, "hidden", axis=1, tiled=True)
    chosen = routes.reshape(-1)
    onehot = (chosen[:, None] == jnp.arange(groups, dtype=jnp.int32)[None, :]).astype(jnp.int32)
    position = jnp.sum((jnp.cumsum(onehot, axis=0) - onehot) * onehot, axis=1)
    target = chosen * capacity + position
    source_row = jnp.arange(token_count * choice_count, dtype=jnp.int32) // choice_count
    payload_width = payload.shape[1]
    outgoing = (
        jnp.zeros((groups * capacity, payload_width), jnp.bfloat16)
        .at[target]
        .set(payload[source_row])
    )
    outgoing = outgoing.reshape(groups, capacity, payload_width)
    gate_matrix = gate_weight[0]
    up_matrix = up_weight[0]
    down_matrix = down_weight[0]
    arrived = lax.all_to_all(outgoing, "expert", split_axis=0, concat_axis=0, tiled=True)
    slot_count = arrived.shape[1]
    inputs = arrived.reshape(groups * slot_count, arrived.shape[2])
    gate_part = jnp.dot(inputs, gate_matrix, preferred_element_type=jnp.float32)
    up_part = jnp.dot(inputs, up_matrix, preferred_element_type=jnp.float32)
    activation = (jax.nn.silu(gate_part) * up_part).astype(jnp.bfloat16)
    answer = jnp.dot(
        lax.all_gather(activation, "hidden", axis=1, tiled=True),
        down_matrix,
        preferred_element_type=jnp.float32,
    ).astype(jnp.bfloat16)
    answer = answer.reshape(groups, slot_count, down_matrix.shape[1])
    returned_rows = lax.all_to_all(answer, "expert", split_axis=0, concat_axis=0, tiled=True)
    returned_rows = returned_rows.reshape(groups * capacity, returned_rows.shape[2])
    picked = returned_rows[target].astype(jnp.float32).reshape(token_count, choice_count, -1)
    combined = jnp.sum(picked * gates[:, :, None], axis=1).astype(jnp.bfloat16)
    combined_all = lax.all_gather(combined, "hidden", axis=1, tiled=True)
    columns = combined_all
    return jnp.dot(
        columns,
        lax.all_gather(dec_weight, "expert", axis=0, tiled=True),
        preferred_element_type=jnp.float32,
    ).astype(jnp.bfloat16)


CORES, LINES = 2, 2
MESH = pl.DeviceIdType.MESH


CHUNKS, HALVES, PAIR, PIECES, STEPS = 2, 2, 2, 4, 2
LATENT_FIRST = ((1, 0), (1, 0), (1, 0), (1, 0))
ANSWER_FIRST = ((0, 1), (0, 1), (0, 1), (0, 1))


def layer_kernel(
    tokens_hbm, enc_hbm, routes, gates, gate_hbm, up_hbm, down_hbm, dec_hbm, out,
    tok, gate, up, down, enc_all, dec_all, latents, table, shares_in, shares, acc, part_out, part_in, activation,
    answers, core_in, one_out, one_in, two_out, two_in, keep, own, z_out, z_in, combined, mixed, part_mixed, mixed_in, result,
    ssem, rsem, lat_z, share_sem, dec_sem, z_sem, local_sem,
):
    groups = lax.axis_size("expert")
    depth = groups // (CORES * LINES)
    e = lax.axis_index("expert")
    h = lax.axis_index("hidden")
    c, y, z = e % CORES, (e // CORES) % LINES, e // (CORES * LINES)

    def at(zz, yy, cc):
        return (zz * LINES + yy) * CORES + cc

    orders = []
    for zz in range(depth):
        others = [o for o in range(depth) if o != zz]
        middle = (depth - 1) / 2
        orders.append([zz] + sorted(others, key=lambda o: (abs(o - zz), abs(o - middle))))
    nearest = []
    for s in range(depth):
        pick = jnp.int32(orders[0][s])
        for zz in range(1, depth):
            pick = jnp.where(z == zz, orders[zz][s], pick)
        nearest.append(pick)

    rows = tok.shape[2] // 2
    wide = tok.shape[3]
    few = latents.shape[2] // groups
    half = latents.shape[3]
    chunk = half // CHUNKS
    band = LINES * CORES * few
    last = depth - 1
    y_peer = (at(z, 1 - y, c), h)
    core_peer = (at(z, y, 1 - c), h)
    x_peer = (e, 1 - h)

    def route(pair, cc):
        along_y = jnp.where(cc == 0, pair[0], pair[1]) == 1
        first = (jnp.where(along_y, at(z, 1 - y, c), e), jnp.where(along_y, h, 1 - h))
        second = (jnp.where(along_y, e, at(z, 1 - y, c)), jnp.where(along_y, 1 - h, h))
        f = (jnp.where(along_y, 1 - y, y), jnp.where(along_y, h, 1 - h))
        g = (jnp.where(along_y, y, 1 - y), jnp.where(along_y, 1 - h, h))
        return first, second, f, g

    waiting, slots, local = [], {}, []

    def slot(*key):
        return rsem.at[slots.setdefault(key, len(slots))]

    def send(src, dst, sem, peer, when=None):
        copy = pltpu.make_async_remote_copy(
            src_ref=src, dst_ref=dst, send_sem=ssem.at[len(waiting)], recv_sem=sem,
            device_id=peer, device_id_type=MESH,
        )
        if when is None:
            copy.start()
        else:
            pl.when(when)(copy.start)
        waiting.append((copy, when))

    def along(zz):
        return (at(jnp.clip(zz, 0, depth - 1), y, c), h)

    def spread(block, sem, far):
        for d in far:
            send(block, block, sem, along(z + d), z + d < depth)
            send(block, block, sem, along(z - d), z - d >= 0)

    def arrive(dst, sem):
        pltpu.make_async_copy(dst, dst, sem).wait()

    def fetch(src, dst):
        copy = pltpu.make_async_copy(src, dst, local_sem.at[len(local)])
        copy.start()
        local.append(copy)
        return copy

    barrier = pltpu.get_barrier_semaphore()
    peers = [((e + d) % groups, h) for d in range(1, groups)] + [x_peer]
    for peer in peers:
        pl.semaphore_signal(barrier, inc=1, device_id=peer, device_id_type=MESH)

    def segment(zz, yy):
        return pl.ds(pl.multiple_of((zz * LINES + yy) * wide, wide), wide)

    enc_own = [
        fetch(enc_hbm.at[:, pl.ds(k * chunk, chunk)], enc_all.at[k, 0, y, c]) for k in range(CHUNKS)
    ]
    pair, twin = z + 1 - 2 * (z % 2), (z + depth // 2) % depth
    planes, pair_planes = (z, twin), (pair, (pair + depth // 2) % depth)
    tok_own = [
        fetch(tokens_hbm.at[:, segment(planes[j], yy)], tok.at[j, yy, pl.ds(0, rows)])
        for j in range(2) for yy in range(LINES)
    ]
    dec_own = fetch(dec_hbm, dec_all.at[z, c])
    part = down.shape[1]
    gate_own = fetch(gate_hbm.at[0], gate)
    up_own = fetch(up_hbm.at[0], up)
    own_down = fetch(down_hbm.at[0, pl.ds(pl.multiple_of(h * part, part), part)], down.at[h])

    expert = lax.broadcasted_iota(jnp.int32, (groups, rows), 0)
    weight = jnp.zeros((groups, rows), jnp.float32)
    for k in range(routes.shape[0]):
        weight += jnp.where(routes[k : k + 1, :] == expert, gates[k : k + 1, :], 0.0)
    for o in range(groups):
        table[o] = jnp.broadcast_to(weight[o : o + 1, :], table.shape[1:])

    pl.semaphore_wait(barrier, len(peers))

    def enc_block(k, j, yy, cc):
        return enc_all.at[k, j, yy, cc]

    def enc_start(k):
        block = enc_block(k, 0, y, c)
        enc_own[k].wait()
        send(block, enc_block(k, 1, y, c), slot("encz", k), along(twin))
        send(block, block, slot("ency", k, 0), y_peer)
        send(block, block, slot("encc", k, 0, 0), core_peer)

    def enc_from_z(k):
        block = enc_block(k, 1, y, c)
        arrive(block, slot("encz", k))
        send(block, block, slot("ency", k, 1), y_peer)
        send(block, block, slot("encc", k, 1, 0), core_peer)

    def enc_from_y(k, j):
        block = enc_block(k, j, 1 - y, c)
        arrive(block, slot("ency", k, j))
        send(block, block, slot("encc", k, j, 1), core_peer)

    def tok_block(j, yy):
        return tok.at[j, yy, pl.ds(rows, rows)]

    def tok_send(j, i):
        yy = y if i == 0 else 1 - y
        send(tokens_hbm.at[:, segment(pair_planes[j], yy)], tok_block(j, yy), slot("tok", j, i), along(pair))

    def tok_wait(j):
        for i, yy in enumerate((y, 1 - y)):
            arrive(tok_block(j, yy), slot("tok", j, i))

    def enc_step(k, j):
        for i, yy in enumerate((y, 1 - y)):
            arrive(enc_block(k, j, yy, 1 - c), slot("encc", k, j, i))
        columns = slice(k * chunk, (k + 1) * chunk)
        for i in range(LINES):
            p = jnp.dot(tok[j, i], enc_all[k, j, i].reshape(wide, chunk), preferred_element_type=jnp.float32)
            if i + j == 0:
                acc[:, columns] = p
            else:
                acc[:, columns] = acc[:, columns] + p

    def enc_share(k):
        part_out[k] = acc[rows + k * few : rows + (k + 1) * few, :].astype(jnp.bfloat16)
        send(part_out.at[k], part_in.at[k], slot("part", k), along(pair))

    def lat_block(k, zz, yy, cc, hh):
        return latents.at[hh, k, pl.ds(pl.multiple_of(at(zz, yy, cc) * few, few), few)]

    def enc_done(k):
        arrive(part_in.at[k], slot("part", k))
        mine = acc[k * few : (k + 1) * few, :] + part_in[k].astype(jnp.float32)
        latents[h, k, pl.ds(pl.multiple_of(e * few, few), few), :] = mine.astype(jnp.bfloat16)
        block = lat_block(k, z, y, c, h)
        spread(block, lat_z.at[k, z], range(1, depth))

    def lat_from_z(k, s):
        zz = nearest[s]
        block = lat_block(k, zz, y, c, h)
        if s > 0:
            arrive(block, lat_z.at[k, zz])
        first, second, _, _ = route(LATENT_FIRST[s % 4], c)
        send(block, block, slot("lat1", k, s), first)
        send(block, block, slot("lat2", k, s), second)
        send(block, block, slot("lat3", k, s, 0), core_peer)

    def lat_from_first(k, s):
        _, second, f, _ = route(LATENT_FIRST[s % 4], c)
        block = lat_block(k, nearest[s], f[0], c, f[1])
        arrive(block, slot("lat1", k, s))
        send(block, block, slot("lat4", k, s), second)
        send(block, block, slot("lat3", k, s, 1), core_peer)

    def lat_from_second(k, s):
        _, _, _, g = route(LATENT_FIRST[s % 4], c)
        block = lat_block(k, nearest[s], g[0], c, g[1])
        arrive(block, slot("lat2", k, s))
        send(block, block, slot("lat3", k, s, 2), core_peer)
        block = lat_block(k, nearest[s], 1 - y, c, 1 - h)
        arrive(block, slot("lat4", k, s))
        send(block, block, slot("lat3", k, s, 3), core_peer)

    def lat_from_core(k, s):
        _, _, f, g = route(LATENT_FIRST[s % 4], 1 - c)
        for i, (yy, hh) in enumerate(((y, h), f, g, (1 - y, 1 - h))):
            arrive(lat_block(k, nearest[s], yy, 1 - c, hh), slot("lat3", k, s, i))

    def dec_block(zz, cc):
        return dec_all.at[zz, cc]

    def dec_middle():
        block, beyond = dec_block(z, c), z - 1 + 2 * (z % 2)
        dec_own.wait()
        send(block, block, dec_sem.at[z], along(beyond), jnp.logical_and(beyond >= 0, beyond < depth))

    def dec_near():
        block = dec_block(z, c)
        send(block, block, dec_sem.at[z], along(pair))
        send(block, block, slot("dec", 0), core_peer)

    def dec_far():
        spread(dec_block(z, c), dec_sem.at[z], range(2, depth))

    def dec_from_z(s):
        zz = nearest[s]
        arrive(dec_block(zz, c), dec_sem.at[zz])
        send(dec_block(zz, c), dec_block(zz, c), slot("dec", s), core_peer)

    def dec_from_core(s):
        arrive(dec_block(nearest[s], 1 - c), slot("dec", s))

    piece = part // PIECES

    def down_rows(hh, i, base):
        return pl.ds(pl.multiple_of(base * part + i * piece, piece), piece)

    def down_send(i):
        send(
            down_hbm.at[0, down_rows(h, i, 1 - h)], down.at[h, pl.ds(i * piece, piece)],
            slot("down", i), x_peer,
        )

    def down_wait():
        own_down.wait()
        for i in range(PIECES):
            arrive(down.at[1 - h, pl.ds(i * piece, piece)], slot("down", i))

    def share_start():
        for d in range(1, groups):
            o = (e + d) % groups
            send(table.at[o], shares_in.at[e], share_sem.at[e], (o, h))
        shares_in[e] = table[e]

    def share_done():
        for d in range(1, groups):
            o = (e + d) % groups
            arrive(shares_in.at[o], share_sem.at[o])
        tiles = [shares_in[nearest[s] * LINES * CORES + b] for s in range(depth) for b in range(LINES * CORES)]
        shares[...] = jnp.concatenate(tiles, axis=0).T

    group = CORES * dec_all.shape[2]
    tile = LINES * group

    stages = [(k, u) for k in range(HALVES) for u in range(depth // PAIR)[:: 1 - 2 * k]]

    def gate_up(s, where):
        k, u = stages[s]
        starts = [pl.multiple_of(nearest[u * PAIR + i] * band, band) for i in range(PAIR)]

        @pl.loop(0, gate.shape[1] // tile)
        def _(n):
            columns = pl.ds(pl.multiple_of(n * tile, tile), tile)
            parts = [
                jnp.concatenate([latents[hh, k, pl.ds(start, band), :] for hh in range(2)], axis=1) for start in starts
            ]
            inputs = jnp.concatenate(parts, axis=0)
            g = jnp.dot(inputs, gate[:, columns], preferred_element_type=jnp.float32)
            u = jnp.dot(inputs, up[:, columns], preferred_element_type=jnp.float32)
            activation[where, :, columns] = (g / (1.0 + jnp.exp(-g)) * u).astype(jnp.bfloat16)

    def answer_rows(s, where):
        k, u = stages[s]
        for i, hh in enumerate((1 - h, h)):
            @pl.loop(0, half // tile)
            def _(n):
                columns = pl.ds(pl.multiple_of(n * tile, tile), tile)
                a = jnp.dot(activation[where], down[hh, :, columns], preferred_element_type=jnp.float32)
                for m in range(PAIR):
                    for b in range(LINES * CORES):
                        start = (m * LINES * CORES + b) * few
                        j = ((u * PAIR + m) * LINES * CORES + b) * 8
                        block = a[start : start + few] * shares[k * few : (k + 1) * few, j : j + 1]
                        for yy in range(LINES):
                            answers[
                                s, b % CORES, yy, hh, pl.ds((m * LINES + b // CORES) * few, few),
                                pl.ds(pl.multiple_of(n * group, group), group),
                            ] = block[:, yy * group : (yy + 1) * group].astype(jnp.bfloat16)

            for yy in range(LINES):
                send(
                    answers.at[s, 1 - c, yy, hh], core_in.at[s, yy, hh], slot("core", s, yy, i), core_peer,
                )

    def both(s, yy, hh):
        return answers[s, c, yy, hh].astype(jnp.float32) + core_in[s, yy, hh].astype(jnp.float32)

    def sum_cores(s):
        first, _, f, _ = route(ANSWER_FIRST[s % 4], c)
        for i, hh in enumerate((1 - h, h)):
            for yy in range(LINES):
                arrive(core_in.at[s, yy, hh], slot("core", s, yy, i))
        for i, (yy, hh) in enumerate(((1 - y, 1 - h), f)):
            one_out[s, i] = both(s, yy, hh).astype(jnp.bfloat16)
            send(one_out.at[s, i], one_in.at[s, i], slot("one", s, i), first)

    def sum_first(s):
        _, second, _, g = route(ANSWER_FIRST[s % 4], c)
        arrive(one_in.at[s, 0], slot("one", s, 0))
        two_out[s] = (both(s, g[0], g[1]) + one_in[s, 0].astype(jnp.float32)).astype(jnp.bfloat16)
        send(two_out.at[s], two_in.at[s], slot("two", s), second)
        arrive(one_in.at[s, 1], slot("one", s, 1))
        keep[s] = both(s, y, h) + one_in[s, 1].astype(jnp.float32)

    def sum_second(s):
        k, u = stages[s]
        arrive(two_in.at[s], slot("two", s))
        total = keep[s] + two_in[s].astype(jnp.float32)
        rest = total.shape[0] // PAIR
        if u == 0:
            own[k] = total[:rest]
        for i in range(PAIR):
            if u + i > 0:
                z_out[s, i] = total[i * rest : (i + 1) * rest].astype(jnp.bfloat16)
                send(z_out.at[s, i], z_in.at[z, k], z_sem.at[z, k], along(nearest[u * PAIR + i]))

    per = depth // 2
    width = part_mixed.shape[3]

    def product(k, hh, columns):
        block = dec_all[pl.ds(pl.multiple_of(hh * per, per), per), :, :, columns].reshape(half // LINES, width)
        return jnp.dot(combined[k, hh], block, preferred_element_type=jnp.float32)

    def combine(k):
        final = own[k]
        for s in range(1, depth):
            arrive(z_in.at[nearest[s], k], z_sem.at[nearest[s], k])
            final += z_in[nearest[s], k].astype(jnp.float32)
        combined[k, h] = final.astype(jnp.bfloat16)
        send(combined.at[k, h], combined.at[k, h], slot("last", k), x_peer)

    def mix(k):
        for n in range(STEPS):
            columns = slice(n * width, (n + 1) * width)
            mixed[k, :, columns] = product(k, h, columns)
        arrive(combined.at[k, 1 - h], slot("last", k))
        theirs = pl.ds(pl.multiple_of((1 - y) * few, few), few)
        for n in range(STEPS):
            columns = slice(n * width, (n + 1) * width)
            mixed[k, :, columns] = mixed[k, :, columns] + product(k, 1 - h, columns)
            part_mixed[k, n] = mixed[k, theirs, columns].astype(jnp.bfloat16)
            send(part_mixed.at[k, n], mixed_in.at[k, n], slot("mixed", k, n), y_peer)

    stored = []

    def store(k):
        mine = pl.ds(pl.multiple_of(y * few, few), few)
        for n in range(STEPS):
            columns = slice(n * width, (n + 1) * width)
            arrive(mixed_in.at[k, n], slot("mixed", k, n))
            result[k, :, columns] = (mixed[k, mine, columns] + mixed_in[k, n].astype(jnp.float32)).astype(jnp.bfloat16)
            window = (pl.ds(k * few, few), pl.ds(n * width, width))
            stored.append(fetch(result.at[k, :, pl.ds(n * width, width)], out.at[window]))

    tok_send(0, 0)
    enc_start(0)
    tok_send(0, 1)
    for i in range(PIECES):
        down_send(i)
    share_start()
    enc_start(1)
    tok_send(1, 0)
    tok_send(1, 1)
    for copy in tok_own:
        copy.wait()
    enc_from_y(0, 0)
    enc_from_z(0)
    enc_from_y(1, 0)
    enc_from_y(0, 1)
    tok_wait(0)
    enc_step(0, 0)
    enc_step(1, 0)
    enc_from_z(1)
    dec_middle()
    enc_from_y(1, 1)
    tok_wait(1)
    enc_step(0, 1)
    enc_step(1, 1)
    enc_share(0)
    enc_share(1)
    enc_done(0)
    lat_from_z(0, 0)
    enc_done(1)
    lat_from_z(1, 0)
    dec_near()
    dec_far()
    lat_from_first(0, 0)
    lat_from_z(0, 1)
    lat_from_first(1, 0)
    lat_from_z(0, 2)
    lat_from_first(0, 1)
    lat_from_z(0, 3)
    share_done()
    gate_own.wait()
    up_own.wait()
    lat_from_second(0, 0)
    lat_from_first(0, 2)
    lat_from_second(0, 1)
    lat_from_z(1, 1)
    lat_from_core(0, 0)
    lat_from_core(0, 1)
    gate_up(0, 0)
    lat_from_z(1, 2)
    lat_from_first(0, 3)
    lat_from_first(1, 1)
    lat_from_z(1, 3)
    lat_from_second(0, 2)
    down_wait()
    answer_rows(0, 0)
    lat_from_first(1, 2)
    lat_from_second(0, 3)
    lat_from_second(1, 0)
    lat_from_second(1, 1)
    lat_from_first(1, 3)
    sum_cores(0)
    lat_from_core(0, 2)
    lat_from_core(0, 3)
    gate_up(1, 1)
    lat_from_second(1, 2)
    lat_from_second(1, 3)
    answer_rows(1, 1)
    sum_first(0)
    lat_from_core(1, 2)
    lat_from_core(1, 3)
    sum_cores(1)
    gate_up(2, 0)
    sum_second(0)
    answer_rows(2, 0)
    lat_from_core(1, 0)
    lat_from_core(1, 1)
    sum_first(1)
    sum_cores(2)
    gate_up(3, 1)
    sum_second(1)
    answer_rows(3, 1)
    sum_first(2)
    sum_cores(3)
    for s in range(1, depth):
        dec_from_z(s)
    sum_second(2)
    sum_first(3)
    combine(0)
    for s in range(depth):
        dec_from_core(s)
    sum_second(3)
    mix(0)
    combine(1)
    mix(1)
    store(0)
    store(1)

    for copy, when in waiting:
        if when is None:
            copy.wait_send()
        else:
            pl.when(when)(copy.wait_send)
    for copy in stored:
        copy.wait()


def whole_layer(tokens, enc_weight, routes, gates, gate_weight, up_weight, down_weight, dec_weight):
    groups = lax.axis_size("expert")
    depth = groups // (CORES * LINES)
    rows, width = tokens.shape
    half = enc_weight.shape[1]
    hidden = gate_weight.shape[2]
    bf, f32 = jnp.bfloat16, jnp.float32
    band = LINES * CORES
    chunk = half // CHUNKS
    few = rows // HALVES
    columns = dec_weight.shape[1]
    block = (PAIR * LINES * few, half // LINES)
    small = (LINES * few, half // LINES)
    anywhere = pl.BlockSpec(memory_space=pl.ANY)
    vmem = pl.BlockSpec(memory_space=pltpu.VMEM)
    dma = pltpu.SemaphoreType.DMA
    scratch = [
        pltpu.VMEM((2, LINES, 2 * rows, width // (LINES * depth)), bf),
        pltpu.VMEM(gate_weight.shape[1:], bf),
        pltpu.VMEM(up_weight.shape[1:], bf),
        pltpu.VMEM((2, hidden, half), bf),
        pltpu.VMEM((CHUNKS, 2, LINES, CORES, enc_weight.shape[0], chunk), bf),
        pltpu.VMEM((depth, CORES, *dec_weight.shape), bf),
        pltpu.VMEM((2, HALVES, groups * few, half), bf),
        pltpu.VMEM((groups, 8, rows), f32),
        pltpu.VMEM((groups, 8, rows), f32),
        pltpu.VMEM((rows, groups * 8), f32),
        pltpu.VMEM((2 * rows, half), f32),
        pltpu.VMEM((HALVES, few, half), bf),
        pltpu.VMEM((HALVES, few, half), bf),
        pltpu.VMEM((2, PAIR * band * few, hidden), bf),
        pltpu.VMEM((depth, CORES, LINES, 2, *block), bf),
        pltpu.VMEM((depth, LINES, 2, *block), bf),
        pltpu.VMEM((depth, 2, *block), bf),
        pltpu.VMEM((depth, 2, *block), bf),
        pltpu.VMEM((depth, *block), bf),
        pltpu.VMEM((depth, *block), bf),
        pltpu.VMEM((depth, *block), f32),
        pltpu.VMEM((HALVES, *small), f32),
        pltpu.VMEM((depth, PAIR, *small), bf),
        pltpu.VMEM((depth, HALVES, *small), bf),
        pltpu.VMEM((HALVES, 2, *small), bf),
        pltpu.VMEM((HALVES, LINES * few, columns), f32),
        pltpu.VMEM((HALVES, STEPS, few, columns // STEPS), bf),
        pltpu.VMEM((HALVES, STEPS, few, columns // STEPS), bf),
        pltpu.VMEM((HALVES, few, columns), bf),
        dma((256,)), dma((160,)), dma((HALVES, depth)),
        dma((groups,)), dma((depth,)), dma((depth, HALVES)), dma((16,)),
    ]
    return pl.pallas_call(
        layer_kernel,
        out_shape=jax.ShapeDtypeStruct((rows, dec_weight.shape[1]), bf),
        in_specs=[anywhere, anywhere, vmem, vmem, anywhere, anywhere, anywhere, anywhere],
        out_specs=anywhere,
        scratch_shapes=scratch,
        compiler_params=pltpu.CompilerParams(
            collective_id=0, has_side_effects=True, vmem_limit_bytes=60 * 1024 * 1024
        ),
    )(tokens, enc_weight, routes.T, gates.T, gate_weight, up_weight, down_weight, dec_weight)


def on_device(tokens, enc_weight, routes, *rest):
    token_count, choice_count = routes.shape
    plan = whole_layer if 2 * choice_count >= lax.axis_size("expert") else exchange_slots
    return plan(tokens, enc_weight, routes, *rest)


def solution(mesh):
    in_specs = (
        P("expert", None),
        P("expert", "hidden"),
        P("expert", None),
        P("expert", None),
        P("expert", None, "hidden"),
        P("expert", None, "hidden"),
        P("expert", None, "hidden"),
        P("expert", "hidden"),
    )
    out_specs = P("expert", "hidden")
    return jax.shard_map(
        on_device, mesh=mesh, in_specs=in_specs, out_specs=out_specs, check_vma=False
    )
```

time: 108 us -> 99.3 us (0.919)
  Pallas kernels: 106 us -> 97.2 us
    pallas_call x1, Pallas kernels: 106 us -> 97.2 us  [whole_layer(): pl.pallas_call(layer_kernel, out_shape=jax.ShapeDtypeStruct((rows, dec_we...]
where the time goes in v2:
time: 99.3 us; the launch traced here: 99.1 us
  Pallas kernels  97.2 us (98%)
  local copies, waits for them, and re-layouts  1.88 us (2%)
    pallas_call x1, Pallas kernels, whole_layer(): pl.pallas_call(layer_kernel, out_shape=jax.ShapeDtypeStruct((rows, dec_we...  97.2 us

profile of v2, /device:TPU:0, one launch (start us, length us, event | category | flops | bytes accessed | tf_op | source)
XLA Modules:
  0.0 99.1 jit_solution(12384096043320136212)
XLA Ops:
  0.0 97.2 %shard_map.82 = bf16[128,2048]{1,0:T(8,128)(2,1)} custom-call(bf16[128,4096]{1,0:T(8,128)(2,1)} %tokens_hbm.1, bf16[256,512]{1,0:T(8,128)(2,1)} %enc_hbm.1, s32[8,128]{1,0:T(8,128)} %bitcast.2, f32[8,128]{1,0:T(8,128)} %bitcast.3, bf16[1,1024,768]{2,1,0:T(8,128)(2,1)} %gate_hbm.1, bf16[1,1024,768]{2,1,0:T(8,128)(2,1)} %up_hbm.1, ...), custom_call_target="tpu_custom_call" | custom-call | tf_op jit(solution)/shard_map/pallas_call | solution.py:589
  97.2 1.9 %copy.10 = bf16[128,2048]{1,0:T(8,128)(2,1)} copy(bf16[128,2048]{1,0:T(8,128)(2,1)} %shard_map.82) | data formatting | bytes 1048576

commit v3 on v2

v3 whole, which is shorter than its diff:
```python
import jax
import jax.numpy as jnp
from jax import lax
from jax.experimental import pallas as pl
from jax.experimental.pallas import tpu as pltpu
from jax.sharding import PartitionSpec as P


def exchange_slots(tokens, enc_weight, routes, gates, gate_weight, up_weight, down_weight, dec_weight):
    groups = lax.axis_size("expert")
    token_count, choice_count = routes.shape
    capacity = min(token_count, 2 * token_count * choice_count // groups)
    columns = tokens
    latent = jnp.dot(
        columns,
        lax.all_gather(enc_weight, "expert", axis=0, tiled=True),
        preferred_element_type=jnp.float32,
    ).astype(jnp.bfloat16)
    payload = lax.all_gather(latent, "hidden", axis=1, tiled=True)
    chosen = routes.reshape(-1)
    onehot = (chosen[:, None] == jnp.arange(groups, dtype=jnp.int32)[None, :]).astype(jnp.int32)
    position = jnp.sum((jnp.cumsum(onehot, axis=0) - onehot) * onehot, axis=1)
    target = chosen * capacity + position
    source_row = jnp.arange(token_count * choice_count, dtype=jnp.int32) // choice_count
    payload_width = payload.shape[1]
    outgoing = (
        jnp.zeros((groups * capacity, payload_width), jnp.bfloat16)
        .at[target]
        .set(payload[source_row])
    )
    outgoing = outgoing.reshape(groups, capacity, payload_width)
    gate_matrix = gate_weight[0]
    up_matrix = up_weight[0]
    down_matrix = down_weight[0]
    arrived = lax.all_to_all(outgoing, "expert", split_axis=0, concat_axis=0, tiled=True)
    slot_count = arrived.shape[1]
    inputs = arrived.reshape(groups * slot_count, arrived.shape[2])
    gate_part = jnp.dot(inputs, gate_matrix, preferred_element_type=jnp.float32)
    up_part = jnp.dot(inputs, up_matrix, preferred_element_type=jnp.float32)
    activation = (jax.nn.silu(gate_part) * up_part).astype(jnp.bfloat16)
    answer = jnp.dot(
        lax.all_gather(activation, "hidden", axis=1, tiled=True),
        down_matrix,
        preferred_element_type=jnp.float32,
    ).astype(jnp.bfloat16)
    answer = answer.reshape(groups, slot_count, down_matrix.shape[1])
    returned_rows = lax.all_to_all(answer, "expert", split_axis=0, concat_axis=0, tiled=True)
    returned_rows = returned_rows.reshape(groups * capacity, returned_rows.shape[2])
    picked = returned_rows[target].astype(jnp.float32).reshape(token_count, choice_count, -1)
    combined = jnp.sum(picked * gates[:, :, None], axis=1).astype(jnp.bfloat16)
    combined_all = lax.all_gather(combined, "hidden", axis=1, tiled=True)
    columns = combined_all
    return jnp.dot(
        columns,
        lax.all_gather(dec_weight, "expert", axis=0, tiled=True),
        preferred_element_type=jnp.float32,
    ).astype(jnp.bfloat16)


CORES, LINES = 2, 2
MESH = pl.DeviceIdType.MESH


CHUNKS, HALVES, PARTS, PIECES, STEPS, RING = 2, 2, 2, 1, 2, 48
LATENT_FIRST = ((1, 0), (1, 0), (1, 0), (1, 0))
ANSWER_FIRST = ((0, 1), (0, 1), (0, 1), (0, 1))


def layer_kernel(
    tokens_hbm, enc_hbm, routes, gates, gate_hbm, up_hbm, down_hbm, dec_hbm, out,
    tok, gate, up, down, enc_all, dec_all, latents, table, shares_in, shares, acc, part_out, part_in, activation,
    answers, core_in, one_out, one_in, two_out, two_in, keep, z_out, z_in, combined, mixed, part_mixed, mixed_in, result,
    ssem, rsem, lat_z, local_sem,
):
    groups = lax.axis_size("expert")
    depth = groups // (CORES * LINES)
    e = lax.axis_index("expert")
    h = lax.axis_index("hidden")
    c, y, z = e % CORES, (e // CORES) % LINES, e // (CORES * LINES)

    def at(zz, yy, cc):
        return (zz * LINES + yy) * CORES + cc

    orders = []
    for zz in range(depth):
        others = [o for o in range(depth) if o != zz]
        middle = (depth - 1) / 2
        orders.append([zz] + sorted(others, key=lambda o: (abs(o - zz), abs(o - middle))))
    nearest = []
    for s in range(depth):
        pick = jnp.int32(orders[0][s])
        for zz in range(1, depth):
            pick = jnp.where(z == zz, orders[zz][s], pick)
        nearest.append(pick)

    rows = tok.shape[2] // 2
    wide = tok.shape[3]
    few, half = latents.shape[3:]
    bit = few // PARTS
    chunk = half // CHUNKS
    last = depth - 1
    y_peer = (at(z, 1 - y, c), h)
    core_peer = (at(z, y, 1 - c), h)
    x_peer = (e, 1 - h)

    def route(pair, cc):
        along_y = jnp.where(cc == 0, pair[0], pair[1]) == 1
        first = (jnp.where(along_y, at(z, 1 - y, c), e), jnp.where(along_y, h, 1 - h))
        second = (jnp.where(along_y, e, at(z, 1 - y, c)), jnp.where(along_y, 1 - h, h))
        f = (jnp.where(along_y, 1 - y, y), jnp.where(along_y, h, 1 - h))
        g = (jnp.where(along_y, y, 1 - y), jnp.where(along_y, 1 - h, h))
        return first, second, f, g

    waiting, lasting, slots, local = [], [], {}, []

    def slot(*key):
        return rsem.at[slots.setdefault(key, len(slots))]

    def sent(copy, when):
        if when is None:
            copy.wait_send()
        else:
            pl.when(when)(copy.wait_send)

    def send(src, dst, sem, peer, when=None, long=False):
        turn = len(waiting)
        if not long and turn >= RING:
            sent(*waiting[turn - RING])
        copy = pltpu.make_async_remote_copy(
            src_ref=src, dst_ref=dst, send_sem=ssem.at[RING + len(lasting) if long else turn % RING], recv_sem=sem,
            device_id=peer, device_id_type=MESH,
        )
        if when is None:
            copy.start()
        else:
            pl.when(when)(copy.start)
        (lasting if long else waiting).append((copy, when))

    def along(zz):
        return (at(jnp.clip(zz, 0, depth - 1), y, c), h)

    def spread(block, sem, far, long=False):
        for d in far:
            send(block, block, sem, along(z + d), z + d < depth, long)
            send(block, block, sem, along(z - d), z - d >= 0, long)

    def arrive(dst, sem):
        pltpu.make_async_copy(dst, dst, sem).wait()

    def fetch(src, dst):
        copy = pltpu.make_async_copy(src, dst, local_sem.at[len(local)])
        copy.start()
        local.append(copy)
        return copy

    barrier = pltpu.get_barrier_semaphore()
    peers = [((e + d) % groups, h) for d in range(1, groups)] + [x_peer]
    for peer in peers:
        pl.semaphore_signal(barrier, inc=1, device_id=peer, device_id_type=MESH)

    def segment(zz, yy):
        return pl.ds(pl.multiple_of((zz * LINES + yy) * wide, wide), wide)

    enc_own = [
        fetch(enc_hbm.at[:, pl.ds(k * chunk, chunk)], enc_all.at[k, 0, y, c]) for k in range(CHUNKS)
    ]
    pair, twin = z + 1 - 2 * (z % 2), (z + depth // 2) % depth
    planes, pair_planes = (z, twin), (pair, (pair + depth // 2) % depth)
    tok_own = [
        fetch(tokens_hbm.at[:, segment(planes[j], yy)], tok.at[j, yy, pl.ds(0, rows)])
        for j in range(2) for yy in range(LINES)
    ]
    dec_own = fetch(dec_hbm, dec_all.at[z, c])
    part = down.shape[1]
    gate_own = fetch(gate_hbm.at[0], gate)
    up_own = fetch(up_hbm.at[0], up)
    own_down = fetch(down_hbm.at[0, pl.ds(pl.multiple_of(h * part, part), part)], down.at[h])

    expert = lax.broadcasted_iota(jnp.int32, (groups, rows), 0)
    weight = jnp.zeros((groups, rows), jnp.float32)
    for k in range(routes.shape[0]):
        weight += jnp.where(routes[k : k + 1, :] == expert, gates[k : k + 1, :], 0.0)
    for o in range(groups):
        table[o] = jnp.broadcast_to(weight[o : o + 1, :], table.shape[1:])

    pl.semaphore_wait(barrier, len(peers))

    def enc_block(k, j, yy, cc):
        return enc_all.at[k, j, yy, cc]

    def enc_start(k):
        block = enc_block(k, 0, y, c)
        enc_own[k].wait()
        send(block, enc_block(k, 1, y, c), slot("encz", k), along(twin))
        send(block, block, slot("ency", k, 0), y_peer)
        send(block, block, slot("encc", k, 0), core_peer)

    def enc_from_z(k):
        block = enc_block(k, 1, y, c)
        arrive(block, slot("encz", k))
        send(block, block, slot("ency", k, 1), y_peer)
        send(block, block, slot("encc", k, 1), core_peer)

    def enc_from_y(k, j):
        block = enc_block(k, j, 1 - y, c)
        arrive(block, slot("ency", k, j))
        send(block, block, slot("encc", k, j), core_peer)

    def tok_block(j, yy):
        return tok.at[j, yy, pl.ds(rows, rows)]

    def tok_send(j, i):
        yy = y if i == 0 else 1 - y
        send(tokens_hbm.at[:, segment(pair_planes[j], yy)], tok_block(j, yy), slot("tok", j), along(pair))

    def tok_wait(j):
        arrive(tok.at[j, :, pl.ds(rows, rows)], slot("tok", j))

    def enc_step(k, j):
        arrive(enc_all.at[k, j, :, 1 - c], slot("encc", k, j))
        columns = slice(k * chunk, (k + 1) * chunk)
        for i in range(LINES):
            p = jnp.dot(tok[j, i], enc_all[k, j, i].reshape(wide, chunk), preferred_element_type=jnp.float32)
            if i + j == 0:
                acc[:, columns] = p
            else:
                acc[:, columns] = acc[:, columns] + p

    def enc_share(k):
        part_out[k] = acc[rows + k * few : rows + (k + 1) * few, :].astype(jnp.bfloat16)
        send(part_out.at[k], part_in.at[k], slot("part", k), along(pair))

    def lat_block(k, zz, yy, cc, hh):
        return latents.at[hh, k, (zz * CORES + cc) * LINES + yy]

    def enc_done(k):
        arrive(part_in.at[k], slot("part", k))
        mine = acc[k * few : (k + 1) * few, :] + part_in[k].astype(jnp.float32)
        latents[h, k, (z * CORES + c) * LINES + y] = mine.astype(jnp.bfloat16)
        block = lat_block(k, z, y, c, h)
        spread(block, lat_z.at[k, z], range(1, depth))

    def lat_from_z(k, s):
        zz = nearest[s]
        block = lat_block(k, zz, y, c, h)
        if s > 0:
            arrive(block, lat_z.at[k, zz])
        first, second, _, _ = route(LATENT_FIRST[s % 4], c)
        send(block, block, slot("lat1", k, s), first)
        send(block, block, slot("lat2", k, s), second)
        send(block, block, slot("lat3", k, s), core_peer)

    def lat_from_first(k, s):
        _, second, f, _ = route(LATENT_FIRST[s % 4], c)
        block = lat_block(k, nearest[s], f[0], c, f[1])
        arrive(block, slot("lat1", k, s))
        send(block, block, slot("lat4", k, s), second)
        send(block, block, slot("lat3", k, s), core_peer)

    def lat_from_second(k, s):
        _, _, _, g = route(LATENT_FIRST[s % 4], c)
        block = lat_block(k, nearest[s], g[0], c, g[1])
        arrive(block, slot("lat2", k, s))
        send(block, block, slot("lat3", k, s), core_peer)
        block = lat_block(k, nearest[s], 1 - y, c, 1 - h)
        arrive(block, slot("lat4", k, s))
        send(block, block, slot("lat3", k, s), core_peer)

    def lat_from_core(k, s):
        start = (nearest[s] * CORES + 1 - c) * LINES
        arrive(latents.at[:, k, pl.ds(start, LINES)], slot("lat3", k, s))

    def dec_block(zz, cc):
        return dec_all.at[zz, cc]

    def dec_middle():
        block, beyond = dec_block(z, c), z - 1 + 2 * (z % 2)
        dec_own.wait()
        send(block, block, slot("decz"), along(beyond), jnp.logical_and(beyond >= 0, beyond < depth), True)

    def dec_near():
        block = dec_block(z, c)
        send(block, block, slot("decz"), along(pair), None, True)
        send(block, block, slot("dec"), core_peer)

    def dec_far():
        spread(dec_block(z, c), slot("decz"), range(2, depth), True)

    def dec_from_z():
        arrive(dec_all.at[pl.ds(0, last), c], slot("decz"))
        for s in range(1, depth):
            block = dec_block(nearest[s], c)
            send(block, block, slot("dec"), core_peer)

    def dec_from_core():
        arrive(dec_all.at[:, 1 - c], slot("dec"))

    piece = part // PIECES

    def down_rows(hh, i, base):
        return pl.ds(pl.multiple_of(base * part + i * piece, piece), piece)

    def down_send(i):
        send(
            down_hbm.at[0, down_rows(h, i, 1 - h)], down.at[h, pl.ds(i * piece, piece)],
            slot("down", i), x_peer, None, True,
        )

    def down_wait():
        own_down.wait()
        for i in range(PIECES):
            arrive(down.at[1 - h, pl.ds(i * piece, piece)], slot("down", i))

    def share_start():
        for d in range(1, groups):
            o = (e + d) % groups
            send(table.at[o], shares_in.at[e], slot("share"), (o, h))
        shares_in[e] = table[e]

    def share_done():
        arrive(shares_in.at[pl.ds(0, groups - 1)], slot("share"))
        shares[...] = jnp.concatenate([shares_in[o] for o in range(groups)], axis=0).T

    group = CORES * dec_all.shape[2]
    tile = LINES * group

    stages = [(k, p) for k in range(HALVES) for p in range(PARTS)]

    def gate_up(s):
        k, p = stages[s]

        @pl.loop(0, gate.shape[1] // tile)
        def _(n):
            columns = pl.ds(pl.multiple_of(n * tile, tile), tile)
            parts = [
                latents[hh, k, :, p * bit : (p + 1) * bit, :].reshape(groups * bit, half) for hh in range(2)
            ]
            inputs = jnp.concatenate(parts, axis=1)
            g = jnp.dot(inputs, gate[:, columns], preferred_element_type=jnp.float32)
            u = jnp.dot(inputs, up[:, columns], preferred_element_type=jnp.float32)
            activation[s % 2, :, columns] = (g / (1.0 + jnp.exp(-g)) * u).astype(jnp.bfloat16)

    def answer_rows(s):
        k, p = stages[s]
        for hh in (1 - h, h):
            @pl.loop(0, half // tile)
            def _(n):
                columns = pl.ds(pl.multiple_of(n * tile, tile), tile)
                a = jnp.dot(activation[s % 2], down[hh, :, columns], preferred_element_type=jnp.float32)
                for b in range(groups):
                    zz, cc, ty = b // (CORES * LINES), b // LINES % CORES, b % LINES
                    j = at(zz, ty, cc) * 8
                    share = shares[k * few + p * bit : k * few + (p + 1) * bit, j : j + 1]
                    block = a[b * bit : (b + 1) * bit] * share
                    for yy in range(LINES):
                        answers[
                            s, cc, yy, hh, pl.ds((zz * LINES + ty) * bit, bit),
                            pl.ds(pl.multiple_of(n * group, group), group),
                        ] = block[:, yy * group : (yy + 1) * group].astype(jnp.bfloat16)

            for yy in range(LINES):
                send(answers.at[s, 1 - c, yy, hh], core_in.at[s, yy, hh], slot("core", s), core_peer)

    def both(s, yy, hh):
        return answers[s, c, yy, hh].astype(jnp.float32) + core_in[s, yy, hh].astype(jnp.float32)

    def sum_cores(s):
        first, _, f, _ = route(ANSWER_FIRST[s % 4], c)
        arrive(core_in.at[s], slot("core", s))
        for i, (yy, hh) in enumerate(((1 - y, 1 - h), f)):
            one_out[s, i] = both(s, yy, hh).astype(jnp.bfloat16)
            send(one_out.at[s, i], one_in.at[s, i], slot("one", s), first)

    def sum_first(s):
        _, second, _, g = route(ANSWER_FIRST[s % 4], c)
        arrive(one_in.at[s], slot("one", s))
        two_out[s] = (both(s, g[0], g[1]) + one_in[s, 0].astype(jnp.float32)).astype(jnp.bfloat16)
        send(two_out.at[s], two_in.at[s], slot("two", s), second)
        keep[s] = both(s, y, h) + one_in[s, 1].astype(jnp.float32)

    def plane_rows(zz):
        return pl.ds(pl.multiple_of(zz * LINES * bit, LINES * bit), LINES * bit)

    def sum_second(s):
        arrive(two_in.at[s], slot("two", s))
        total = keep[s] + two_in[s].astype(jnp.float32)
        keep[s] = total
        z_out[s] = total.astype(jnp.bfloat16)
        for i in range(last, 0, -1):
            send(z_out.at[s, plane_rows(nearest[i])], z_in.at[s, z], slot("z", s), along(nearest[i]))

    per = depth // 2
    width = part_mixed.shape[3]

    def product(s, hh, columns):
        block = dec_all[pl.ds(pl.multiple_of(hh * per, per), per), :, :, columns].reshape(half // LINES, width)
        return jnp.dot(combined[s, hh], block, preferred_element_type=jnp.float32)

    def combine(s):
        arrive(z_in.at[s, pl.ds(0, last)], slot("z", s))
        final = keep[s, plane_rows(z)]
        for i in range(1, depth):
            final += z_in[s, nearest[i]].astype(jnp.float32)
        combined[s, h] = final.astype(jnp.bfloat16)
        send(combined.at[s, h], combined.at[s, h], slot("last", s), x_peer)

    def mix(s):
        for n in range(STEPS):
            columns = slice(n * width, (n + 1) * width)
            mixed[s, :, columns] = product(s, h, columns)
        arrive(combined.at[s, 1 - h], slot("last", s))
        theirs = pl.ds(pl.multiple_of((1 - y) * bit, bit), bit)
        for n in range(STEPS):
            columns = slice(n * width, (n + 1) * width)
            mixed[s, :, columns] = mixed[s, :, columns] + product(s, 1 - h, columns)
            part_mixed[s, n] = mixed[s, theirs, columns].astype(jnp.bfloat16)
            send(part_mixed.at[s, n], mixed_in.at[s, n], slot("mixed", s, n), y_peer)

    stored = []

    def store(s):
        mine = pl.ds(pl.multiple_of(y * bit, bit), bit)
        for n in range(STEPS):
            columns = slice(n * width, (n + 1) * width)
            arrive(mixed_in.at[s, n], slot("mixed", s, n))
            result[s, :, columns] = (mixed[s, mine, columns] + mixed_in[s, n].astype(jnp.float32)).astype(jnp.bfloat16)
        stored.append(fetch(result.at[s], out.at[pl.ds(s * bit, bit)]))

    tok_send(0, 0)
    enc_start(0)
    tok_send(0, 1)
    for i in range(PIECES):
        down_send(i)
    share_start()
    enc_start(1)
    tok_send(1, 0)
    tok_send(1, 1)
    for copy in tok_own:
        copy.wait()
    enc_from_y(0, 0)
    enc_from_z(0)
    enc_from_y(1, 0)
    enc_from_y(0, 1)
    tok_wait(0)
    enc_step(0, 0)
    enc_step(1, 0)
    enc_from_z(1)
    dec_middle()
    enc_from_y(1, 1)
    tok_wait(1)
    enc_step(0, 1)
    enc_step(1, 1)
    enc_share(0)
    enc_share(1)
    enc_done(0)
    lat_from_z(0, 0)
    enc_done(1)
    lat_from_z(1, 0)
    dec_near()
    dec_far()
    lat_from_first(0, 0)
    lat_from_z(0, 1)
    lat_from_first(1, 0)
    lat_from_z(0, 2)
    lat_from_first(0, 1)
    lat_from_z(0, 3)
    share_done()
    gate_own.wait()
    up_own.wait()
    lat_from_second(0, 0)
    lat_from_first(0, 2)
    lat_from_z(1, 1)
    lat_from_second(0, 1)
    lat_from_first(0, 3)
    lat_from_z(1, 2)
    lat_from_second(0, 2)
    lat_from_first(1, 1)
    lat_from_z(1, 3)
    lat_from_second(0, 3)
    for s in range(depth):
        lat_from_core(0, s)
    gate_up(0)
    lat_from_first(1, 2)
    down_wait()
    answer_rows(0)
    lat_from_first(1, 3)
    lat_from_second(1, 0)
    lat_from_second(1, 1)
    gate_up(1)
    sum_cores(0)
    lat_from_second(1, 2)
    lat_from_second(1, 3)
    answer_rows(1)
    for s in range(depth):
        lat_from_core(1, s)
    gate_up(2)
    sum_cores(1)
    answer_rows(2)
    sum_first(0)
    gate_up(3)
    sum_cores(2)
    dec_from_z()
    answer_rows(3)
    sum_first(1)
    sum_cores(3)
    sum_second(0)
    sum_first(2)
    sum_second(1)
    dec_from_core()
    sum_first(3)
    combine(0)
    sum_second(2)
    combine(1)
    mix(0)
    sum_second(3)
    mix(1)
    combine(2)
    combine(3)
    mix(2)
    mix(3)
    for s in range(len(stages)):
        store(s)

    for copy, when in lasting + waiting[-RING:]:
        sent(copy, when)
    for copy in stored:
        copy.wait()


def whole_layer(tokens, enc_weight, routes, gates, gate_weight, up_weight, down_weight, dec_weight):
    groups = lax.axis_size("expert")
    depth = groups // (CORES * LINES)
    rows, width = tokens.shape
    half = enc_weight.shape[1]
    hidden = gate_weight.shape[2]
    bf, f32 = jnp.bfloat16, jnp.float32
    band = LINES * CORES
    chunk = half // CHUNKS
    few = rows // HALVES
    columns = dec_weight.shape[1]
    bit = few // PARTS
    stages = HALVES * PARTS
    block = (depth * LINES * bit, half // LINES)
    small = (LINES * bit, half // LINES)
    anywhere = pl.BlockSpec(memory_space=pl.ANY)
    vmem = pl.BlockSpec(memory_space=pltpu.VMEM)
    dma = pltpu.SemaphoreType.DMA
    scratch = [
        pltpu.VMEM((2, LINES, 2 * rows, width // (LINES * depth)), bf),
        pltpu.VMEM(gate_weight.shape[1:], bf),
        pltpu.VMEM(up_weight.shape[1:], bf),
        pltpu.VMEM((2, hidden, half), bf),
        pltpu.VMEM((CHUNKS, 2, LINES, CORES, enc_weight.shape[0], chunk), bf),
        pltpu.VMEM((depth, CORES, *dec_weight.shape), bf),
        pltpu.VMEM((2, HALVES, groups, few, half), bf),
        pltpu.VMEM((groups, 8, rows), f32),
        pltpu.VMEM((groups, 8, rows), f32),
        pltpu.VMEM((rows, groups * 8), f32),
        pltpu.VMEM((2 * rows, half), f32),
        pltpu.VMEM((HALVES, few, half), bf),
        pltpu.VMEM((HALVES, few, half), bf),
        pltpu.VMEM((2, groups * bit, hidden), bf),
        pltpu.VMEM((stages, CORES, LINES, 2, *block), bf),
        pltpu.VMEM((stages, LINES, 2, *block), bf),
        pltpu.VMEM((stages, 2, *block), bf),
        pltpu.VMEM((stages, 2, *block), bf),
        pltpu.VMEM((stages, *block), bf),
        pltpu.VMEM((stages, *block), bf),
        pltpu.VMEM((stages, *block), f32),
        pltpu.VMEM((stages, *block), bf),
        pltpu.VMEM((stages, depth, *small), bf),
        pltpu.VMEM((stages, 2, *small), bf),
        pltpu.VMEM((stages, LINES * bit, columns), f32),
        pltpu.VMEM((stages, STEPS, bit, columns // STEPS), bf),
        pltpu.VMEM((stages, STEPS, bit, columns // STEPS), bf),
        pltpu.VMEM((stages, bit, columns), bf),
        dma((RING + 7,)), dma((80,)), dma((HALVES, depth)), dma((18,)),
    ]
    return pl.pallas_call(
        layer_kernel,
        out_shape=jax.ShapeDtypeStruct((rows, dec_weight.shape[1]), bf),
        in_specs=[anywhere, anywhere, vmem, vmem, anywhere, anywhere, anywhere, anywhere],
        out_specs=anywhere,
        scratch_shapes=scratch,
        compiler_params=pltpu.CompilerParams(
            collective_id=0, has_side_effects=True, vmem_limit_bytes=60 * 1024 * 1024
        ),
    )(tokens, enc_weight, routes.T, gates.T, gate_weight, up_weight, down_weight, dec_weight)


def on_device(tokens, enc_weight, routes, *rest):
    token_count, choice_count = routes.shape
    plan = whole_layer if 2 * choice_count >= lax.axis_size("expert") else exchange_slots
    return plan(tokens, enc_weight, routes, *rest)


def solution(mesh):
    in_specs = (
        P("expert", None),
        P("expert", "hidden"),
        P("expert", None),
        P("expert", None),
        P("expert", None, "hidden"),
        P("expert", None, "hidden"),
        P("expert", None, "hidden"),
        P("expert", "hidden"),
    )
    out_specs = P("expert", "hidden")
    return jax.shard_map(
        on_device, mesh=mesh, in_specs=in_specs, out_specs=out_specs, check_vma=False
    )
```

time: 99.3 us -> 95 us (0.957)
  Pallas kernels: 97.2 us -> 92.9 us
    pallas_call x1, Pallas kernels: 97.2 us -> 92.9 us  [whole_layer(): pl.pallas_call(layer_kernel, out_shape=jax.ShapeDtypeStruct((rows, dec_we...]
where the time goes in v3:
time: 95 us; the launch traced here: 94.8 us
  Pallas kernels  92.9 us (98%)
  local copies, waits for them, and re-layouts  1.88 us (2%)
    pallas_call x1, Pallas kernels, whole_layer(): pl.pallas_call(layer_kernel, out_shape=jax.ShapeDtypeStruct((rows, dec_we...  92.9 us

profile of v3, /device:TPU:0, one launch (start us, length us, event | category | flops | bytes accessed | tf_op | source)
XLA Modules:
  0.0 94.8 jit_solution(48113379371146984)
XLA Ops:
  0.0 92.9 %shard_map.82 = bf16[128,2048]{1,0:T(8,128)(2,1)} custom-call(bf16[128,4096]{1,0:T(8,128)(2,1)} %tokens_hbm.1, bf16[256,512]{1,0:T(8,128)(2,1)} %enc_hbm.1, s32[8,128]{1,0:T(8,128)} %bitcast.2, f32[8,128]{1,0:T(8,128)} %bitcast.3, bf16[1,1024,768]{2,1,0:T(8,128)(2,1)} %gate_hbm.1, bf16[1,1024,768]{2,1,0:T(8,128)(2,1)} %up_hbm.1, ...), custom_call_target="tpu_custom_call" | custom-call | tf_op jit(solution)/shard_map/pallas_call | solution.py:579
  92.9 1.9 %copy.10 = bf16[128,2048]{1,0:T(8,128)(2,1)} copy(bf16[128,2048]{1,0:T(8,128)(2,1)} %shard_map.82) | data formatting | bytes 1048576

commit v4 on v3

--- a/solution.py
+++ b/solution.py
@@ -237,6 +237,8 @@
         arrive(part_in.at[k], slot("part", k))
         mine = acc[k * few : (k + 1) * few, :] + part_in[k].astype(jnp.float32)
         latents[h, k, (z * CORES + c) * LINES + y] = mine.astype(jnp.bfloat16)
+
+    def lat_spread(k):
         block = lat_block(k, z, y, c, h)
         spread(block, lat_z.at[k, z], range(1, depth))
 
@@ -329,7 +331,7 @@
     def gate_up(s):
         k, p = stages[s]
 
-        @pl.loop(0, gate.shape[1] // tile)
+        @pl.loop(0, gate.shape[1] // tile, unroll=True)
         def _(n):
             columns = pl.ds(pl.multiple_of(n * tile, tile), tile)
             parts = [
@@ -343,7 +345,7 @@
     def answer_rows(s):
         k, p = stages[s]
         for hh in (1 - h, h):
-            @pl.loop(0, half // tile)
+            @pl.loop(0, half // tile, unroll=True)
             def _(n):
                 columns = pl.ds(pl.multiple_of(n * tile, tile), tile)
                 a = jnp.dot(activation[s % 2], down[hh, :, columns], preferred_element_type=jnp.float32)
@@ -453,15 +455,15 @@
     enc_share(0)
     enc_share(1)
     enc_done(0)
+    lat_spread(0)
     lat_from_z(0, 0)
     enc_done(1)
     lat_from_z(1, 0)
-    dec_near()
-    dec_far()
     lat_from_first(0, 0)
     lat_from_z(0, 1)
     lat_from_first(1, 0)
     lat_from_z(0, 2)
+    lat_spread(1)
     lat_from_first(0, 1)
     lat_from_z(0, 3)
     share_done()
@@ -476,6 +478,8 @@
     lat_from_second(0, 2)
     lat_from_first(1, 1)
     lat_from_z(1, 3)
+    dec_near()
+    dec_far()
     lat_from_second(0, 3)
     for s in range(depth):
         lat_from_core(0, s)
@@ -499,24 +503,24 @@
     sum_first(0)
     gate_up(3)
     sum_cores(2)
-    dec_from_z()
     answer_rows(3)
     sum_first(1)
     sum_cores(3)
     sum_second(0)
     sum_first(2)
     sum_second(1)
+    dec_from_z()
+    sum_first(3)
     dec_from_core()
-    sum_first(3)
     combine(0)
     sum_second(2)
     combine(1)
+    sum_second(3)
     mix(0)
-    sum_second(3)
     mix(1)
     combine(2)
+    mix(2)
     combine(3)
-    mix(2)
     mix(3)
     for s in range(len(stages)):
         store(s)

time: 95 us -> 93.2 us (0.981)
  Pallas kernels: 92.9 us -> 91.1 us
    pallas_call x1, Pallas kernels: 92.9 us -> 91.1 us  [whole_layer(): pl.pallas_call(layer_kernel, out_shape=jax.ShapeDtypeStruct((rows, dec_we...]
where the time goes in v4:
time: 93.2 us; the launch traced here: 93 us
  Pallas kernels  91.1 us (98%)
  local copies, waits for them, and re-layouts  1.88 us (2%)
    pallas_call x1, Pallas kernels, whole_layer(): pl.pallas_call(layer_kernel, out_shape=jax.ShapeDtypeStruct((rows, dec_we...  91.1 us
    unnamed x1, local copies, waits for them, and re-layouts  1.88 us

profile of v4, /device:TPU:0, one launch (start us, length us, event | category | flops | bytes accessed | tf_op | source)
XLA Modules:
  0.0 93.0 jit_solution(16345403403527085044)
XLA Ops:
  0.0 91.1 %shard_map.82 = bf16[128,2048]{1,0:T(8,128)(2,1)} custom-call(bf16[128,4096]{1,0:T(8,128)(2,1)} %tokens_hbm.1, bf16[256,512]{1,0:T(8,128)(2,1)} %enc_hbm.1, s32[8,128]{1,0:T(8,128)} %bitcast.2, f32[8,128]{1,0:T(8,128)} %bitcast.3, bf16[1,1024,768]{2,1,0:T(8,128)(2,1)} %gate_hbm.1, bf16[1,1024,768]{2,1,0:T(8,128)(2,1)} %up_hbm.1, ...), custom_call_target="tpu_custom_call" | custom-call | tf_op jit(solution)/shard_map/pallas_call | solution.py:583
  91.1 1.9 %copy.10 = bf16[128,2048]{1,0:T(8,128)(2,1)} copy(bf16[128,2048]{1,0:T(8,128)(2,1)} %shard_map.82) | data formatting | bytes 1048576

commit v5 on v4

--- a/solution.py
+++ b/solution.py
@@ -61,7 +61,7 @@
 MESH = pl.DeviceIdType.MESH
 
 
-CHUNKS, HALVES, PARTS, PIECES, STEPS, RING = 2, 2, 2, 1, 2, 48
+CHUNKS, HALVES, PARTS, PIECES, STEPS, RING = 2, 2, 2, 1, 2, 40
 LATENT_FIRST = ((1, 0), (1, 0), (1, 0), (1, 0))
 ANSWER_FIRST = ((0, 1), (0, 1), (0, 1), (0, 1))
 
@@ -433,13 +433,13 @@
     tok_send(0, 1)
     for i in range(PIECES):
         down_send(i)
-    share_start()
     enc_start(1)
     tok_send(1, 0)
     tok_send(1, 1)
     for copy in tok_own:
         copy.wait()
     enc_from_y(0, 0)
+    share_start()
     enc_from_z(0)
     enc_from_y(1, 0)
     enc_from_y(0, 1)
@@ -504,8 +504,8 @@
     gate_up(3)
     sum_cores(2)
     answer_rows(3)
+    sum_cores(3)
     sum_first(1)
-    sum_cores(3)
     sum_second(0)
     sum_first(2)
     sum_second(1)
@@ -578,7 +578,7 @@
         pltpu.VMEM((stages, STEPS, bit, columns // STEPS), bf),
         pltpu.VMEM((stages, STEPS, bit, columns // STEPS), bf),
         pltpu.VMEM((stages, bit, columns), bf),
-        dma((RING + 7,)), dma((80,)), dma((HALVES, depth)), dma((18,)),
+        dma((RING + 7,)), dma((78,)), dma((HALVES, depth)), dma((14,)),
     ]
     return pl.pallas_call(
         layer_kernel,

time: 93.2 us -> 92.6 us (level)
  no operation moved by 1% of the time
where the time goes in v5:
time: 92.6 us; the launch traced here: 92.4 us
  Pallas kernels  90.5 us (98%)
  local copies, waits for them, and re-layouts  1.88 us (2%)
    pallas_call x1, Pallas kernels, whole_layer(): pl.pallas_call(layer_kernel, out_shape=jax.ShapeDtypeStruct((rows, dec_we...  90.5 us
    unnamed x1, local copies, waits for them, and re-layouts  1.88 us

profile of v5, /device:TPU:0, one launch (start us, length us, event | category | flops | bytes accessed | tf_op | source)
XLA Modules:
  0.0 92.4 jit_solution(12440701056543688378)
XLA Ops:
  0.0 90.5 %shard_map.82 = bf16[128,2048]{1,0:T(8,128)(2,1)} custom-call(bf16[128,4096]{1,0:T(8,128)(2,1)} %tokens_hbm.1, bf16[256,512]{1,0:T(8,128)(2,1)} %enc_hbm.1, s32[8,128]{1,0:T(8,128)} %bitcast.2, f32[8,128]{1,0:T(8,128)} %bitcast.3, bf16[1,1024,768]{2,1,0:T(8,128)(2,1)} %gate_hbm.1, bf16[1,1024,768]{2,1,0:T(8,128)(2,1)} %up_hbm.1, ...), custom_call_target="tpu_custom_call" | custom-call | tf_op jit(solution)/shard_map/pallas_call | solution.py:583
  90.5 1.9 %copy.10 = bf16[128,2048]{1,0:T(8,128)(2,1)} copy(bf16[128,2048]{1,0:T(8,128)(2,1)} %shard_map.82) | data formatting | bytes 1048576
